TPU v7x, 256 devices: a whole 4x4x8 slice. The times are simulated.
256 devices in a mesh: gx: 8 (over z_hi, core), gy: 16 (over y, x), gz: 2 (over z_lo).
Axes of the slice: x: 4, y: 4, z: 8 (z_hi: 4, z_lo: 2; z = z_hi * 2 + z_lo), core: 2. Of those that a mesh axis runs over, the one named last changes fastest.
Arguments:
- right_side: float32 [64, 512, 512], P('gx', 'gy', 'gz'), may hold values from -4 to 4
- volscale: float32 [64, 512, 512], P('gx', 'gy', 'gz'), may hold values from 0.5 to 2
Outputs:
- solution: float32 [64, 512, 512], P('gx', 'gy', 'gz')
- residual: float32 [64, 512, 512], P('gx', 'gy', 'gz')
All inputs are finite; a program needn't handle non-finite values.
Results may differ from a plain program's by a relative error of at most 0.000047.
Values sent between devices are 32-bit elements; how exact they have to be, the bound alone decides.
A program may use at most 64 MiB of HBM per device.

v0:
```python
import jax
import jax.numpy as jnp
from jax import lax
from jax.sharding import PartitionSpec as P

diffusion_rates = (48.0, 40.0, 32.0)
cross_rates = (8.0, 6.0, -6.0)
drift_rates = (3.0, -2.0, 1.5)
total_rate = 120.0
discount = 0.05
damping = 0.6


def extended(cells, sides, width):
    for axis, dim in sides:
        count = lax.axis_size(axis)
        ends = count - 1
        head = lax.slice_in_dim(cells, 0, width, axis=dim)
        tail = lax.slice_in_dim(cells, cells.shape[dim] - width, cells.shape[dim], axis=dim)
        cells = jnp.concatenate(
            [
                lax.ppermute(tail, axis, [(i, (i + 1) % count) for i in range(ends)]),
                cells,
                lax.ppermute(head, axis, [((i + 1) % count, i) for i in range(ends)]),
            ],
            axis=dim,
        )
    return cells


def operate(padded, local_scale, spacing):
    extent = local_scale.shape

    def shifted(offset):
        starts = tuple((1 + offset[dim_index] for dim_index in range(3)))
        stops = tuple((starts[dim_index] + extent[dim_index] for dim_index in range(3)))
        return lax.slice(padded, starts, stops)

    center = shifted((0, 0, 0))
    curvature_factor = 1.0 / (spacing * spacing)
    slope_factor = 0.5 / spacing
    second = jnp.zeros_like(center)
    slopes = jnp.zeros_like(center)
    for dim_index in range(3):
        forward = shifted(tuple((1 if other == dim_index else 0 for other in range(3))))
        backward = shifted(tuple((-1 if other == dim_index else 0 for other in range(3))))
        second = second + diffusion_rates[dim_index] * curvature_factor * (
            forward + backward - 2.0 * center
        )
        slopes = slopes + drift_rates[dim_index] * slope_factor * (forward - backward)
    pairs_list = ((0, 1), (0, 2), (1, 2))
    for pair_index in range(3):
        first_axis, second_axis = pairs_list[pair_index]

        def corner(sign_first, sign_second):
            offset = [0, 0, 0]
            offset[first_axis] = sign_first
            offset[second_axis] = sign_second
            return shifted(tuple(offset))

        mixed = corner(1, 1) - corner(1, -1) - corner(-1, 1) + corner(-1, -1)
        second = second + cross_rates[pair_index] * 0.25 * curvature_factor * mixed
    return (1.0 + discount) * center - local_scale * second - slopes


def diagonal_of(local_scale, spacing):
    return 1.0 + discount + 2.0 * total_rate * local_scale / (spacing * spacing)


def relax_step(current, applied, source, local_scale, spacing):
    return current + damping * (source - applied) / diagonal_of(local_scale, spacing)


def coarsen(values):
    size_x, size_y, size_z = values.shape
    return (
        values.reshape(size_x // 2, 2, size_y // 2, 2, size_z // 2, 2).sum(axis=(1, 3, 5)) * 0.125
    )


def refine(values):
    size_x, size_y, size_z = values.shape
    copies = jnp.broadcast_to(values[:, None, :, None, :, None], (size_x, 2, size_y, 2, size_z, 2))
    return copies.reshape(2 * size_x, 2 * size_y, 2 * size_z)


def fine_image(current, volscale):
    padded = extended(current, (("gx", 0), ("gy", 1), ("gz", 2)), 1)
    return operate(padded, volscale, 1.0)


def on_device(right_side, volscale):

    def two_sweeps(current):
        for sweep_index in range(2):
            current = relax_step(current, fine_image(current, volscale), right_side, volscale, 1.0)
        return current

    smoothed = two_sweeps(right_side)
    residue = right_side - fine_image(smoothed, volscale)
    coarse_rhs = coarsen(residue)
    coarse_scale = coarsen(volscale)
    whole_rhs, whole_scale = (
        lax.all_gather(coarse_rhs, "gz", axis=2, tiled=True),
        lax.all_gather(coarse_scale, "gz", axis=2, tiled=True),
    )
    correction = damping * whole_rhs / diagonal_of(whole_scale, 2.0)
    for sweep_index in range(3):
        bordered = extended(correction, (("gx", 0), ("gy", 1)), 1)
        padded = jnp.pad(bordered, ((0, 0), (0, 0), (1, 1)))
        correction = relax_step(
            correction, operate(padded, whole_scale, 2.0), whole_rhs, whole_scale, 2.0
        )
    coarse_depth = coarse_rhs.shape[2]
    correction = lax.dynamic_slice_in_dim(
        correction, lax.axis_index("gz") * coarse_depth, coarse_depth, 2
    )
    solution = two_sweeps(smoothed + refine(correction))
    residual = right_side - fine_image(solution, volscale)
    return (solution, residual)


def solution(mesh):
    placed = (P("gx", "gy", "gz"), P("gx", "gy", "gz"))
    return jax.shard_map(
        on_device,
        mesh=mesh,
        in_specs=placed,
        out_specs=(P("gx", "gy", "gz"), P("gx", "gy", "gz")),
        check_vma=False,
    )
```

profile of v0, /device:TPU:184, one launch (start us, length us, event | category | flops | bytes accessed | tf_op | source)
XLA Modules:
  0.0 318.8 jit_solution(11174067661156123354)
XLA Ops:
  3.3 5.8 %collective-permute-start = (f32[1,32,256]{2,1,0:T(8,128)S(1)}, f32[1,32,256]{2,1,0:T(8,128)S(1)}, u32[]{:S(2)}, u32[]{:S(2)}) collective-permute-start(f32[1,32,256]{2,1,0:T(8,128)S(1)} %get-tuple-element.60), channel_id=1, source_target_pairs={{32,0},{64,32},{96,64},{128,96},{160,128},{192,160},{224,192},{33,... | collective-permute-start | bytes 98312 | tf_op jit(solution)/shard_map/ppermute | solution.py:24
  10.7 4.8 %collective-permute-start.2 = (f32[10,1,256]{2,1,0:T(1,128)S(1)}, f32[10,1,256]{2,1,0:T(1,128)S(1)}, u32[]{:S(2)}, u32[]{:S(2)}) collective-permute-start(f32[10,1,256]{2,1,0:T(1,128)S(1)} %get-tuple-element.48), channel_id=1, source_target_pairs={{2,0},{4,2},{6,4},{8,6},{10,8},{12,10},{14,12},{16,14},{18,16},{20... | collective-permute-start | bytes 30728 | tf_op jit(solution)/shard_map/ppermute | solution.py:24
  17.5 5.7 %collective-permute-done.3 = f32[10,1,256]{2,1,0:T(1,128)S(1)} collective-permute-done((f32[10,1,256]{2,1,0:T(1,128)S(1)}, f32[10,1,256]{2,1,0:T(1,128)S(1)}, u32[]{:S(2)}, u32[]{:S(2)}) %collective-permute-start.3) | collective-permute-done | bytes 10272 | tf_op jit(solution)/shard_map/ppermute | solution.py:22
  41.2 5.4 %collective-permute-done.7 = f32[1,32,256]{2,1,0:T(8,128)S(1)} collective-permute-done((f32[1,32,256]{2,1,0:T(8,128)S(1)}, f32[1,32,256]{2,1,0:T(8,128)S(1)}, u32[]{:S(2)}, u32[]{:S(2)}) %collective-permute-start.7) | collective-permute-done | bytes 32800 | tf_op jit(solution)/shard_map/ppermute | solution.py:22
  52.6 18.8 %reshape.15 = f32[4,2,16,2,128,2]{5,4,3,2,1,0:T(8,128)} reshape(f32[8,32,256]{2,1,0:T(8,128)} %param.3) | data formatting | bytes 524288 | tf_op jit(solution)/shard_map/reshape | solution.py:77
  71.5 7.0 %reduce_sum.19 = f32[4,16,128]{2,1,0:T(8,128)S(1)} reduce(f32[4,2,16,2,128,2]{5,4,3,2,1,0:T(8,128)} %reshape.15, f32[]{:T(128)} %constant.8.clone.1), dimensions={1,3,5}, to_apply=%region_1.0 | reduce | flops 57344 | bytes 294916 | tf_op jit(solution)/shard_map/reduce_sum | solution.py:77
  83.7 4.4 %collective-permute-done.11 = f32[10,34,1]{2,1,0:T(8,128)S(1)} collective-permute-done((f32[10,34,1]{2,1,0:T(8,128)S(1)}, f32[10,34,1]{2,1,0:T(8,128)S(1)}, u32[]{:S(2)}, u32[]{:S(2)}) %collective-permute-start.11) | collective-permute-done | bytes 1392 | tf_op jit(solution)/shard_map/ppermute | solution.py:22
  93.4 4.9 %collective-permute-done.13 = f32[1,32,256]{2,1,0:T(8,128)S(1)} collective-permute-done((f32[1,32,256]{2,1,0:T(8,128)S(1)}, f32[1,32,256]{2,1,0:T(8,128)S(1)}, u32[]{:S(2)}, u32[]{:S(2)}) %collective-permute-start.13) | collective-permute-done | bytes 32800 | tf_op jit(solution)/shard_map/ppermute | solution.py:22
  104.3 4.6 %all_gather.7 = f32[4,16,256]{2,1,0:T(8,128)S(1)} all-gather(f32[4,16,128]{2,1,0:T(8,128)S(1)} %broadcast_multiply_fusion.1), channel_id=1, replica_groups=mesh['gx'=8,'gy'=16,'gz'=2] {'gz'}, dimensions={2}, use_global_device_ids=true | all-gather | bytes 98304 | tf_op jit(solution)/shard_map/all_gather | solution.py:105
  114.9 4.4 %collective-permute-done.17 = f32[10,34,1]{2,1,0:T(8,128)S(1)} collective-permute-done((f32[10,34,1]{2,1,0:T(8,128)S(1)}, f32[10,34,1]{2,1,0:T(8,128)S(1)}, u32[]{:S(2)}, u32[]{:S(2)}) %collective-permute-start.17) | collective-permute-done | bytes 1392 | tf_op jit(solution)/shard_map/ppermute | solution.py:22
  120.2 18.1 %reshape.14 = f32[4,2,16,2,128,2]{5,4,3,2,1,0:T(8,128)} reshape(f32[8,32,256]{2,1,0:T(8,128)S(1)} %fusion.59) | data formatting | bytes 524288 | tf_op jit(solution)/shard_map/reshape | solution.py:77
  138.3 7.0 %reduce_sum.18 = f32[4,16,128]{2,1,0:T(8,128)S(1)} reduce(f32[4,2,16,2,128,2]{5,4,3,2,1,0:T(8,128)} %reshape.14, f32[]{:T(128)} %constant.8.clone.1), dimensions={1,3,5}, to_apply=%region_0.0 | reduce | flops 57344 | bytes 294916 | tf_op jit(solution)/shard_map/reduce_sum | solution.py:77
  145.3 4.6 %all_gather.6 = f32[4,16,256]{2,1,0:T(8,128)S(1)} all-gather(f32[4,16,128]{2,1,0:T(8,128)S(1)} %broadcast_multiply_fusion.2), channel_id=1, replica_groups=mesh['gx'=8,'gy'=16,'gz'=2] {'gz'}, dimensions={2}, use_global_device_ids=true | all-gather | bytes 98304 | tf_op jit(solution)/shard_map/all_gather | solution.py:104
  154.3 4.7 %collective-permute-done.19 = f32[1,16,256]{2,1,0:T(8,128)S(1)} collective-permute-done((f32[1,16,256]{2,1,0:T(8,128)S(1)}, f32[1,16,256]{2,1,0:T(8,128)S(1)}, u32[]{:S(2)}, u32[]{:S(2)}) %collective-permute-start.19) | collective-permute-done | bytes 16416 | tf_op jit(solution)/shard_map/ppermute | solution.py:22
  159.1 5.7 %collective-permute-start.20 = (f32[6,1,256]{2,1,0:T(1,128)S(1)}, f32[6,1,256]{2,1,0:T(1,128)S(1)}, u32[]{:S(2)}, u32[]{:S(2)}) collective-permute-start(f32[6,1,256]{2,1,0:T(1,128)S(1)} %get-tuple-element.73), channel_id=1, source_target_pairs={{2,0},{4,2},{6,4},{8,6},{10,8},{12,10},{14,12},{16,14},{18,16},{20... | collective-permute-start | bytes 18440 | tf_op jit(solution)/shard_map/ppermute | solution.py:24
  166.7 5.7 %collective-permute-done.21 = f32[6,1,256]{2,1,0:T(1,128)S(1)} collective-permute-done((f32[6,1,256]{2,1,0:T(1,128)S(1)}, f32[6,1,256]{2,1,0:T(1,128)S(1)}, u32[]{:S(2)}, u32[]{:S(2)}) %collective-permute-start.21) | collective-permute-done | bytes 6176 | tf_op jit(solution)/shard_map/ppermute | solution.py:22
  177.1 4.7 %collective-permute-done.23 = f32[1,16,256]{2,1,0:T(8,128)S(1)} collective-permute-done((f32[1,16,256]{2,1,0:T(8,128)S(1)}, f32[1,16,256]{2,1,0:T(8,128)S(1)}, u32[]{:S(2)}, u32[]{:S(2)}) %collective-permute-start.23) | collective-permute-done | bytes 16416 | tf_op jit(solution)/shard_map/ppermute | solution.py:22
  196.2 4.7 %collective-permute-done.27 = f32[1,16,256]{2,1,0:T(8,128)S(1)} collective-permute-done((f32[1,16,256]{2,1,0:T(8,128)S(1)}, f32[1,16,256]{2,1,0:T(8,128)S(1)}, u32[]{:S(2)}, u32[]{:S(2)}) %collective-permute-start.27) | collective-permute-done | bytes 16416 | tf_op jit(solution)/shard_map/ppermute | solution.py:22
  211.0 6.5 %broadcast_in_dim.2 = f32[4,2,16,2,128,2]{5,4,3,2,1,0:T(8,128)} broadcast(f32[4,16,128]{2,1,0:T(8,128)S(1)} %dynamic-slice_add_fusion), dimensions={0,2,4} | broadcast | bytes 294912 | tf_op jit(solution)/shard_map/broadcast_in_dim | solution.py:83
  217.5 12.7 %reshape.16 = f32[8,32,256]{2,1,0:T(8,128)S(1)} reshape(f32[4,2,16,2,128,2]{5,4,3,2,1,0:T(8,128)} %broadcast_in_dim.2) | data formatting | bytes 524288 | tf_op jit(solution)/shard_map/reshape | solution.py:84
  234.7 4.9 %collective-permute-done.31 = f32[1,32,256]{2,1,0:T(8,128)S(1)} collective-permute-done((f32[1,32,256]{2,1,0:T(8,128)S(1)}, f32[1,32,256]{2,1,0:T(8,128)S(1)}, u32[]{:S(2)}, u32[]{:S(2)}) %collective-permute-start.31) | collective-permute-done | bytes 32800 | tf_op jit(solution)/shard_map/ppermute | solution.py:22
  254.5 4.4 %collective-permute-done.35 = f32[10,34,1]{2,1,0:T(8,128)S(1)} collective-permute-done((f32[10,34,1]{2,1,0:T(8,128)S(1)}, f32[10,34,1]{2,1,0:T(8,128)S(1)}, u32[]{:S(2)}, u32[]{:S(2)}) %collective-permute-start.35) | collective-permute-done | bytes 1392 | tf_op jit(solution)/shard_map/ppermute | solution.py:22
  264.2 4.9 %collective-permute-done.37 = f32[1,32,256]{2,1,0:T(8,128)S(1)} collective-permute-done((f32[1,32,256]{2,1,0:T(8,128)S(1)}, f32[1,32,256]{2,1,0:T(8,128)S(1)}, u32[]{:S(2)}, u32[]{:S(2)}) %collective-permute-start.37) | collective-permute-done | bytes 32800 | tf_op jit(solution)/shard_map/ppermute | solution.py:22
  293.4 4.9 %collective-permute-done.43 = f32[1,32,256]{2,1,0:T(8,128)S(1)} collective-permute-done((f32[1,32,256]{2,1,0:T(8,128)S(1)}, f32[1,32,256]{2,1,0:T(8,128)S(1)}, u32[]{:S(2)}, u32[]{:S(2)}) %collective-permute-start.43) | collective-permute-done | bytes 32800 | tf_op jit(solution)/shard_map/ppermute | solution.py:22
  (151 shorter events, 157.8 us)
Async XLA Ops:
  1.4 7.7 %collective-permute-start.1 = (f32[1,32,256]{2,1,0:T(8,128)S(1)}, f32[1,32,256]{2,1,0:T(8,128)S(1)}, u32[]{:S(2)}, u32[]{:S(2)}) collective-permute-start(f32[1,32,256]{2,1,0:T(8,128)S(1)} %get-tuple-element.61), channel_id=1, source_target_pairs={{0,32},{32,64},{64,96},{96,128},{128,160},{160,192},{192,224},{1,3... | collective-permute-start | bytes 98312 | tf_op jit(solution)/shard_map/ppermute | solution.py:22
  15.5 7.7 %collective-permute-start.3 = (f32[10,1,256]{2,1,0:T(1,128)S(1)}, f32[10,1,256]{2,1,0:T(1,128)S(1)}, u32[]{:S(2)}, u32[]{:S(2)}) collective-permute-start(f32[10,1,256]{2,1,0:T(1,128)S(1)} %get-tuple-element.49), channel_id=1, source_target_pairs={{0,2},{2,4},{4,6},{6,8},{8,10},{10,12},{12,14},{14,16},{16,18},{18... | collective-permute-start | bytes 30728 | tf_op jit(solution)/shard_map/ppermute | solution.py:22
  26.3 7.7 %collective-permute-start.5 = (f32[10,34,1]{2,1,0:T(8,128)S(1)}, f32[10,34,1]{2,1,0:T(8,128)S(1)}, u32[]{:S(2)}, u32[]{:S(2)}) collective-permute-start(f32[10,34,1]{2,1,0:T(8,128)S(1)} %get-tuple-element.15), channel_id=1, source_target_pairs={{0,1},{2,3},{4,5},{6,7},{8,9},{10,11},{12,13},{14,15},{16,17},{18,... | collective-permute-start | bytes 4088 | tf_op jit(solution)/shard_map/ppermute | solution.py:22
  39.3 7.3 %collective-permute-start.7 = (f32[1,32,256]{2,1,0:T(8,128)S(1)}, f32[1,32,256]{2,1,0:T(8,128)S(1)}, u32[]{:S(2)}, u32[]{:S(2)}) collective-permute-start(f32[1,32,256]{2,1,0:T(8,128)S(1)} %get-tuple-element.58), channel_id=1, source_target_pairs={{0,32},{32,64},{64,96},{96,128},{128,160},{160,192},{192,224},{1,3... | collective-permute-start | bytes 98312 | tf_op jit(solution)/shard_map/ppermute | solution.py:22
  46.6 31.8 %collective-permute-start.8 = (f32[10,1,256]{2,1,0:T(1,128)S(1)}, f32[10,1,256]{2,1,0:T(1,128)S(1)}, u32[]{:S(2)}, u32[]{:S(2)}) collective-permute-start(f32[10,1,256]{2,1,0:T(1,128)S(1)} %get-tuple-element.47), channel_id=1, source_target_pairs={{2,0},{4,2},{6,4},{8,6},{10,8},{12,10},{14,12},{16,14},{18,16},{20... | collective-permute-start | bytes 30728 | tf_op jit(solution)/shard_map/ppermute | solution.py:24
  48.6 29.9 %collective-permute-start.9 = (f32[10,1,256]{2,1,0:T(1,128)S(1)}, f32[10,1,256]{2,1,0:T(1,128)S(1)}, u32[]{:S(2)}, u32[]{:S(2)}) collective-permute-start(f32[10,1,256]{2,1,0:T(1,128)S(1)} %get-tuple-element.46), channel_id=1, source_target_pairs={{0,2},{2,4},{4,6},{6,8},{8,10},{10,12},{12,14},{14,16},{16,18},{18... | collective-permute-start | bytes 30728 | tf_op jit(solution)/shard_map/ppermute | solution.py:22
  80.4 7.7 %collective-permute-start.11 = (f32[10,34,1]{2,1,0:T(8,128)S(1)}, f32[10,34,1]{2,1,0:T(8,128)S(1)}, u32[]{:S(2)}, u32[]{:S(2)}) collective-permute-start(f32[10,34,1]{2,1,0:T(8,128)S(1)} %get-tuple-element.13), channel_id=1, source_target_pairs={{0,1},{2,3},{4,5},{6,7},{8,9},{10,11},{12,13},{14,15},{16,17},{18,... | collective-permute-start | bytes 4088 | tf_op jit(solution)/shard_map/ppermute | solution.py:22
  91.0 7.3 %collective-permute-start.13 = (f32[1,32,256]{2,1,0:T(8,128)S(1)}, f32[1,32,256]{2,1,0:T(8,128)S(1)}, u32[]{:S(2)}, u32[]{:S(2)}) collective-permute-start(f32[1,32,256]{2,1,0:T(8,128)S(1)} %get-tuple-element.56), channel_id=1, source_target_pairs={{0,32},{32,64},{64,96},{96,128},{128,160},{160,192},{192,224},{1,3... | collective-permute-start | bytes 98312 | tf_op jit(solution)/shard_map/ppermute | solution.py:22
  98.3 10.6 %collective-permute-start.14 = (f32[10,1,256]{2,1,0:T(1,128)S(1)}, f32[10,1,256]{2,1,0:T(1,128)S(1)}, u32[]{:S(2)}, u32[]{:S(2)}) collective-permute-start(f32[10,1,256]{2,1,0:T(1,128)S(1)} %get-tuple-element.43), channel_id=1, source_target_pairs={{2,0},{4,2},{6,4},{8,6},{10,8},{12,10},{14,12},{16,14},{18,16},{20... | collective-permute-start | bytes 30728 | tf_op jit(solution)/shard_map/ppermute | solution.py:24
  102.4 7.7 %collective-permute-start.15 = (f32[10,1,256]{2,1,0:T(1,128)S(1)}, f32[10,1,256]{2,1,0:T(1,128)S(1)}, u32[]{:S(2)}, u32[]{:S(2)}) collective-permute-start(f32[10,1,256]{2,1,0:T(1,128)S(1)} %get-tuple-element.42), channel_id=1, source_target_pairs={{0,2},{2,4},{4,6},{6,8},{8,10},{10,12},{12,14},{14,16},{16,18},{18... | collective-permute-start | bytes 30728 | tf_op jit(solution)/shard_map/ppermute | solution.py:22
  111.7 7.7 %collective-permute-start.17 = (f32[10,34,1]{2,1,0:T(8,128)S(1)}, f32[10,34,1]{2,1,0:T(8,128)S(1)}, u32[]{:S(2)}, u32[]{:S(2)}) collective-permute-start(f32[10,34,1]{2,1,0:T(8,128)S(1)} %get-tuple-element.11), channel_id=1, source_target_pairs={{0,1},{2,3},{4,5},{6,7},{8,9},{10,11},{12,13},{14,15},{16,17},{18,... | collective-permute-start | bytes 4088 | tf_op jit(solution)/shard_map/ppermute | solution.py:22
  159.1 7.6 %collective-permute-start.20 = (f32[6,1,256]{2,1,0:T(1,128)S(1)}, f32[6,1,256]{2,1,0:T(1,128)S(1)}, u32[]{:S(2)}, u32[]{:S(2)}) collective-permute-start(f32[6,1,256]{2,1,0:T(1,128)S(1)} %get-tuple-element.73), channel_id=1, source_target_pairs={{2,0},{4,2},{6,4},{8,6},{10,8},{12,10},{14,12},{16,14},{18,16},{20... | collective-permute-start | bytes 18440 | tf_op jit(solution)/shard_map/ppermute | solution.py:24
  164.7 7.6 %collective-permute-start.21 = (f32[6,1,256]{2,1,0:T(1,128)S(1)}, f32[6,1,256]{2,1,0:T(1,128)S(1)}, u32[]{:S(2)}, u32[]{:S(2)}) collective-permute-start(f32[6,1,256]{2,1,0:T(1,128)S(1)} %get-tuple-element.72), channel_id=1, source_target_pairs={{0,2},{2,4},{4,6},{6,8},{8,10},{10,12},{12,14},{14,16},{16,18},{18... | collective-permute-start | bytes 18440 | tf_op jit(solution)/shard_map/ppermute | solution.py:22
  183.8 7.6 %collective-permute-start.25 = (f32[6,1,256]{2,1,0:T(1,128)S(1)}, f32[6,1,256]{2,1,0:T(1,128)S(1)}, u32[]{:S(2)}, u32[]{:S(2)}) collective-permute-start(f32[6,1,256]{2,1,0:T(1,128)S(1)} %get-tuple-element.68), channel_id=1, source_target_pairs={{0,2},{2,4},{4,6},{6,8},{8,10},{10,12},{12,14},{14,16},{16,18},{18... | collective-permute-start | bytes 18440 | tf_op jit(solution)/shard_map/ppermute | solution.py:22
  202.9 7.6 %collective-permute-start.29 = (f32[6,1,256]{2,1,0:T(1,128)S(1)}, f32[6,1,256]{2,1,0:T(1,128)S(1)}, u32[]{:S(2)}, u32[]{:S(2)}) collective-permute-start(f32[6,1,256]{2,1,0:T(1,128)S(1)} %get-tuple-element.64), channel_id=1, source_target_pairs={{0,2},{2,4},{4,6},{6,8},{8,10},{10,12},{12,14},{14,16},{16,18},{18... | collective-permute-start | bytes 18440 | tf_op jit(solution)/shard_map/ppermute | solution.py:22
  232.2 7.3 %collective-permute-start.31 = (f32[1,32,256]{2,1,0:T(8,128)S(1)}, f32[1,32,256]{2,1,0:T(8,128)S(1)}, u32[]{:S(2)}, u32[]{:S(2)}) collective-permute-start(f32[1,32,256]{2,1,0:T(8,128)S(1)} %get-tuple-element.54), channel_id=1, source_target_pairs={{0,32},{32,64},{64,96},{96,128},{128,160},{160,192},{192,224},{1,3... | collective-permute-start | bytes 98312 | tf_op jit(solution)/shard_map/ppermute | solution.py:22
  241.5 7.7 %collective-permute-start.33 = (f32[10,1,256]{2,1,0:T(1,128)S(1)}, f32[10,1,256]{2,1,0:T(1,128)S(1)}, u32[]{:S(2)}, u32[]{:S(2)}) collective-permute-start(f32[10,1,256]{2,1,0:T(1,128)S(1)} %get-tuple-element.38), channel_id=1, source_target_pairs={{0,2},{2,4},{4,6},{6,8},{8,10},{10,12},{12,14},{14,16},{16,18},{18... | collective-permute-start | bytes 30728 | tf_op jit(solution)/shard_map/ppermute | solution.py:22
  251.3 7.7 %collective-permute-start.35 = (f32[10,34,1]{2,1,0:T(8,128)S(1)}, f32[10,34,1]{2,1,0:T(8,128)S(1)}, u32[]{:S(2)}, u32[]{:S(2)}) collective-permute-start(f32[10,34,1]{2,1,0:T(8,128)S(1)} %get-tuple-element.9), channel_id=1, source_target_pairs={{0,1},{2,3},{4,5},{6,7},{8,9},{10,11},{12,13},{14,15},{16,17},{18,... | collective-permute-start | bytes 4088 | tf_op jit(solution)/shard_map/ppermute | solution.py:22
  261.8 7.3 %collective-permute-start.37 = (f32[1,32,256]{2,1,0:T(8,128)S(1)}, f32[1,32,256]{2,1,0:T(8,128)S(1)}, u32[]{:S(2)}, u32[]{:S(2)}) collective-permute-start(f32[1,32,256]{2,1,0:T(8,128)S(1)} %get-tuple-element.52), channel_id=1, source_target_pairs={{0,32},{32,64},{64,96},{96,128},{128,160},{160,192},{192,224},{1,3... | collective-permute-start | bytes 98312 | tf_op jit(solution)/shard_map/ppermute | solution.py:22
  271.1 7.7 %collective-permute-start.39 = (f32[10,1,256]{2,1,0:T(1,128)S(1)}, f32[10,1,256]{2,1,0:T(1,128)S(1)}, u32[]{:S(2)}, u32[]{:S(2)}) collective-permute-start(f32[10,1,256]{2,1,0:T(1,128)S(1)} %get-tuple-element.34), channel_id=1, source_target_pairs={{0,2},{2,4},{4,6},{6,8},{8,10},{10,12},{12,14},{14,16},{16,18},{18... | collective-permute-start | bytes 30728 | tf_op jit(solution)/shard_map/ppermute | solution.py:22
  280.4 7.7 %collective-permute-start.41 = (f32[10,34,1]{2,1,0:T(8,128)S(1)}, f32[10,34,1]{2,1,0:T(8,128)S(1)}, u32[]{:S(2)}, u32[]{:S(2)}) collective-permute-start(f32[10,34,1]{2,1,0:T(8,128)S(1)} %get-tuple-element.7), channel_id=1, source_target_pairs={{0,1},{2,3},{4,5},{6,7},{8,9},{10,11},{12,13},{14,15},{16,17},{18,... | collective-permute-start | bytes 4088 | tf_op jit(solution)/shard_map/ppermute | solution.py:22
  291.0 7.3 %collective-permute-start.43 = (f32[1,32,256]{2,1,0:T(8,128)S(1)}, f32[1,32,256]{2,1,0:T(8,128)S(1)}, u32[]{:S(2)}, u32[]{:S(2)}) collective-permute-start(f32[1,32,256]{2,1,0:T(8,128)S(1)} %get-tuple-element.50), channel_id=1, source_target_pairs={{0,32},{32,64},{64,96},{96,128},{128,160},{160,192},{192,224},{1,3... | collective-permute-start | bytes 98312 | tf_op jit(solution)/shard_map/ppermute | solution.py:22
  300.3 7.7 %collective-permute-start.45 = (f32[10,1,256]{2,1,0:T(1,128)S(1)}, f32[10,1,256]{2,1,0:T(1,128)S(1)}, u32[]{:S(2)}, u32[]{:S(2)}) collective-permute-start(f32[10,1,256]{2,1,0:T(1,128)S(1)} %get-tuple-element.30), channel_id=1, source_target_pairs={{0,2},{2,4},{4,6},{6,8},{8,10},{10,12},{12,14},{14,16},{16,18},{18... | collective-permute-start | bytes 30728 | tf_op jit(solution)/shard_map/ppermute | solution.py:22
  309.6 7.7 %collective-permute-start.47 = (f32[10,34,1]{2,1,0:T(8,128)S(1)}, f32[10,34,1]{2,1,0:T(8,128)S(1)}, u32[]{:S(2)}, u32[]{:S(2)}) collective-permute-start(f32[10,34,1]{2,1,0:T(8,128)S(1)} %get-tuple-element.5), channel_id=1, source_target_pairs={{0,1},{2,3},{4,5},{6,7},{8,9},{10,11},{12,13},{14,15},{16,17},{18,... | collective-permute-start | bytes 4088 | tf_op jit(solution)/shard_map/ppermute | solution.py:22
  (27 other events, 240.7 us)
where the time goes:
time: 321 us; the launch traced here: 319 us
  starting transfers between devices  117 us (36%)
  waiting for transfers between devices  109 us (34%)
  local copies, waits for them, and re-layouts  58.7 us (18%)
  other arithmetic  23.5 us (7%)
  blocking collectives  9.17 us (3%)
    ppermute x24, waiting for transfers between devices, extended(): lax.ppermute(tail, axis, [(i, (i + 1) % count) for i in range(ends)])  96.6 us
    ppermute x24, starting transfers between devices, extended(): lax.ppermute(head, axis, [((i + 1) % count, i) for i in range(ends)])  59.3 us
    ppermute x24, starting transfers between devices, extended(): lax.ppermute(tail, axis, [(i, (i + 1) % count) for i in range(ends)])  58 us
    reshape x2, local copies, waits for them, and re-layouts, coarsen(): values.reshape(size_x // 2, 2, size_y // 2, 2, size_z // 2, 2)  37 us
    reduce_sum x2, other arithmetic, coarsen(): values.reshape(size_x // 2, 2, size_y // 2, 2, size_z // 2, 2)  14 us
    reshape x1, local copies, waits for them, and re-layouts, refine(): return copies.reshape(2 * size_x, 2 * size_y, 2 * size_z)  12.7 us
    ppermute x24, waiting for transfers between devices, extended(): lax.ppermute(head, axis, [((i + 1) % count, i) for i in range(ends)])  12.1 us
    broadcast_in_dim x1, local copies, waits for them, and re-layouts, refine(): jnp.broadcast_to(values[:, None, :, None, :, None], (size_x, 2, size_y, 2...  6.51 us
  transfers between devices with their start and end apart: 48, of which 29 were waited for; matrix products, arithmetic and copies ran while one was open for 9% of the time, Pallas kernels for 0%

commit v1 on v0

v1 whole, which is shorter than its diff:
```python
import jax
import jax.numpy as jnp
from jax import lax
from jax.experimental import pallas as pl
from jax.experimental.pallas import tpu as pltpu
from jax.sharding import PartitionSpec as P

MESH = pl.DeviceIdType.MESH
F32 = jnp.float32
NXD, NYD = 8, 16
BX, BY = 8, 32
HALO = 5
PX = BX + 2 * HALO
ROWS = BY + 16
CX = BX // 2 + 2 * HALO
CROWS = BY // 2 + 16
DAMP = 0.6


def main_messages():
    out = []
    for dx in (1, -1, 0):
        for dy in (0, 1, -1):
            if dx == 0 and dy == 0:
                continue
            if dy == 0:
                rs, rd = (8, 32), (8, 32)
            elif dy == 1:
                rs, rd = (35, 5), (3, 5)
            else:
                rs, rd = (8, 5), (40, 5)
            if dx == 0:
                for a in (0, 1):
                    out.append((0, dx, dy, a, (5, 8), (5, 8), rs, rd))
            elif dx == 1:
                out.append((0, dx, dy, 0, (10, 3), (2, 3), rs, rd))
                out.append((0, dx, dy, 1, (11, 2), (3, 2), rs, rd))
                out.append((1, dx, dy, 0, (8, 2), (0, 2), rs, rd))
                out.append((1, dx, dy, 1, (9, 2), (1, 2), rs, rd))
            else:
                out.append((0, dx, dy, 0, (5, 3), (13, 3), rs, rd))
                out.append((0, dx, dy, 1, (5, 2), (13, 2), rs, rd))
                out.append((1, dx, dy, 0, (8, 2), (16, 2), rs, rd))
                out.append((1, dx, dy, 1, (7, 2), (15, 2), rs, rd))
    return out


def pack_messages():
    out = []
    for dx in (1, -1, 0):
        for dy in (0, 1, -1):
            ps, pd = {0: ((0, 8), (5, 8)), 1: ((3, 5), (0, 5)), -1: ((0, 5), (13, 5))}[dx]
            rs = {0: (0, 8), 1: (3, 5), -1: (0, 5)}[dy]
            out.append((dx, dy, ps, pd, rs))
    return out


def coarse_messages():
    out = []
    for dz in (0, 1):
        for dx in (1, -1, 2, -2, 0):
            for dy in (0, 1, -1):
                if dx == 0 and dy == 0 and dz == 0:
                    continue
                ps, pd = {
                    0: ((5, 4), (5, 4)),
                    1: ((5, 4), (1, 4)),
                    -1: ((5, 4), (9, 4)),
                    2: ((8, 1), (0, 1)),
                    -2: ((5, 1), (13, 1)),
                }[dx]
                rs, rd = {0: ((8, 16), (8, 16)), 1: ((19, 5), (3, 5)), -1: ((8, 5), (24, 5))}[dy]
                out.append((dx, dy, dz, ps, pd, rs, rd))
    return out


MAIN = main_messages()
PACK = pack_messages()
COARSE = coarse_messages()
NM, NP, NC = len(MAIN), len(PACK), len(COARSE)


def ds(pair):
    return pl.ds(pair[0], pair[1])


def up(x):
    return pltpu.roll(x, 127, 1)


def down(x):
    return pltpu.roll(x, 1, 1)


def shifts(vals, lane, circular):
    count = len(vals)
    ups = [up(v) for v in vals]
    downs = [down(v) for v in vals]
    zero = jnp.zeros_like(vals[0])
    plus, minus = [], []
    for t in range(count):
        nxt = ups[(t + 1) % count] if circular or t + 1 < count else zero
        prv = downs[t - 1] if circular or t > 0 else zero
        plus.append(jnp.where(lane == 127, nxt, ups[t]))
        minus.append(jnp.where(lane == 0, prv, downs[t]))
    return plus, minus


def stencil(ref, p, r, tiles, outs, circular, lane, h):
    sf = 1.0 / (h * h)
    bf = 1.0 / h
    centre, parts, mixed = [], [], []
    for t in range(tiles):
        v = ref[p, t, pl.ds(r, 8), :]
        xm = ref[p - 1, t, pl.ds(r, 8), :]
        xp = ref[p + 1, t, pl.ds(r, 8), :]
        ym = ref[p, t, pl.ds(r - 1, 8), :]
        yp = ref[p, t, pl.ds(r + 1, 8), :]
        d = xp - xm
        fy = yp - ym
        centre.append(v)
        mixed.append(d - fy)
        if t in outs:
            dyy = (ref[p + 1, t, pl.ds(r + 1, 8), :] - ref[p - 1, t, pl.ds(r + 1, 8), :]) - (
                ref[p + 1, t, pl.ds(r - 1, 8), :] - ref[p - 1, t, pl.ds(r - 1, 8), :]
            )
            s = (48.0 * sf) * (xp + xm) + (40.0 * sf) * (yp + ym) + (2.0 * sf) * dyy
            b = (1.5 * bf) * d - bf * fy
        else:
            s = b = None
        parts.append((s, b))
    vp, vm = shifts(centre, lane, circular)
    hp, hm = shifts(mixed, lane, circular)
    result = []
    for t in outs:
        s, b = parts[t]
        s = s + (32.0 * sf) * (vp[t] + vm[t]) + (1.5 * sf) * (hp[t] - hm[t])
        b = b + (0.75 * bf) * (vp[t] - vm[t])
        result.append((centre[t], s, b))
    return result


def kernel(g_hbm, c_hbm, sol_hbm, res_hbm, GC, PS, PR, W, A, B, RX, CO, CW, CA, CB, UPS, OUT,
           load_sem, m_send, m_recv, p_send, p_recv, c_send, c_recv, out_sem):
    gx, gy, gz = lax.axis_index("gx"), lax.axis_index("gy"), lax.axis_index("gz")

    def peer(dx, dy, dz):
        return (
            lax.rem(gx + (dx + NXD), NXD),
            lax.rem(gy + (dy + NYD), NYD),
            lax.rem(gz + dz, 2),
        )

    loads = []
    for a, src in ((0, g_hbm), (1, c_hbm)):
        for t in range(2):
            cp = pltpu.make_async_copy(
                src.at[:, :, pl.ds(128 * t, 128)],
                GC.at[a, pl.ds(5, 8), t, pl.ds(8, 32), :],
                load_sem.at[2 * a + t],
            )
            cp.start()
            loads.append(cp)

    barrier = pltpu.get_barrier_semaphore()
    for dx, dy, dz, *_ in COARSE:
        pl.semaphore_signal(barrier, inc=1, device_id=peer(dx, dy, dz), device_id_type=MESH)

    for cp in loads:
        cp.wait()

    lane = lax.broadcasted_iota(jnp.int32, (8, 128), 1)
    sub = lax.broadcasted_iota(jnp.int32, (8, 128), 0)
    zfirst = 120 * gz
    zmask = (lane >= zfirst) & (lane < zfirst + 8)

    def pack_plane(x, _):
        acc = jnp.zeros((8, 128), F32)
        for a in range(2):
            for j in range(4):
                m = 4 * a + j
                t0 = GC[a, 5 + x, 0, pl.ds(8 + 8 * j, 8), :]
                t1 = GC[a, 5 + x, 1, pl.ds(8 + 8 * j, 8), :]
                both = pltpu.roll(jnp.where(lane >= 64, t1, t0), (16 * m + 8) % 128, 1)
                acc = jnp.where((lane >= 16 * m) & (lane < 16 * m + 16), both, acc)
        PS[x] = acc
        return 0

    lax.fori_loop(0, 8, pack_plane, 0)

    row_i = lax.broadcasted_iota(jnp.int32, (256, 128), 0)
    col_i = lax.broadcasted_iota(jnp.int32, (256, 128), 1)
    pool = jnp.where(row_i // 2 == col_i, 0.125, 0.0).astype(F32)

    def coarsen_rows(k):
        pieces = []
        for i in range(4):
            cols = []
            for t in range(2):
                cols.append(RX[i, t, pl.ds(0, 16, stride=2), :] + RX[i, t, pl.ds(1, 16, stride=2), :])
            pieces.append(jnp.concatenate(cols, axis=1))
        allp = jnp.concatenate(pieces, axis=0)
        q = jnp.dot(allp, pool, preferred_element_type=F32, precision=lax.Precision.HIGHEST)
        for i in range(4):
            CO[k, 5 + i, gz, pl.ds(8, 16), :] = q[16 * i : 16 * i + 16]

    def pair_scale(i, _):
        for t in range(2):
            RX[i, t] = GC[1, 5 + 2 * i, t, pl.ds(8, 32), :] + GC[1, 6 + 2 * i, t, pl.ds(8, 32), :]
        return 0

    lax.fori_loop(0, 4, pair_scale, 0)
    coarsen_rows(1)

    pl.semaphore_wait(barrier, NC)

    def main_copy(i):
        _, dx, dy, a, ps, pd, rs, rd = MAIN[i]
        return pltpu.make_async_remote_copy(
            src_ref=GC.at[a, ds(ps), pl.ds(0, 2), ds(rs), :],
            dst_ref=GC.at[a, ds(pd), pl.ds(0, 2), ds(rd), :],
            send_sem=m_send.at[i],
            recv_sem=m_recv.at[i],
            device_id=peer(dx, dy, 0),
            device_id_type=MESH,
        )

    def pack_copy(i):
        dx, dy, ps, pd, rs = PACK[i]
        return pltpu.make_async_remote_copy(
            src_ref=PS.at[ds(ps), ds(rs), :],
            dst_ref=PR.at[1 - dy, ds(pd), ds(rs), :],
            send_sem=p_send.at[i],
            recv_sem=p_recv.at[i],
            device_id=peer(dx, dy, 1),
            device_id_type=MESH,
        )

    def coarse_copy(k, i, arriving=False):
        dx, dy, dz, ps, pd, rs, rd = COARSE[i]
        tile = lax.rem(gz + dz, 2) if arriving else gz
        return pltpu.make_async_remote_copy(
            src_ref=CO.at[k, ds(ps), tile, ds(rs), :],
            dst_ref=CO.at[k, ds(pd), tile, ds(rd), :],
            send_sem=c_send.at[k * NC + i],
            recv_sem=c_recv.at[k * NC + i],
            device_id=peer(dx, dy, dz),
            device_id_type=MESH,
        )

    early = [i for i in range(NM) if MAIN[i][0] == 0]
    late = [i for i in range(NM) if MAIN[i][0] == 1]
    for i in range(NP):
        pack_copy(i).start()
    for i in early:
        main_copy(i).start()
    for i in late:
        main_copy(i).start()
    for i in range(NC):
        coarse_copy(1, i).start()

    for i in range(NP):
        pack_copy(i).wait_recv()
    for i in early:
        main_copy(i).wait_recv()
    for i in late:
        main_copy(i).wait_recv()

    def unpack_plane(p, _):
        for a in range(2):
            for r in range(6):
                slot, j = (0, 3) if r == 0 else (2, 0) if r == 5 else (1, r - 1)
                m = 4 * a + j
                v = pltpu.roll(PR[slot, p], (128 - 16 * m - 8) % 128, 1)
                GC[a, p, 2, pl.ds(8 * r, 8), :] = jnp.where(zmask, v, 0.0)
        return 0

    lax.fori_loop(0, PX, unpack_plane, 0)

    def clear_planes(first):
        def one(p, _):
            GC[0, p] = jnp.zeros((3, ROWS, 128), F32)
            return 0
        lax.fori_loop(first, first + 5, one, 0)

    def clear_rows(first):
        def one(p, _):
            for t in range(3):
                GC[0, p, t, pl.ds(first, 8), :] = jnp.zeros((8, 128), F32)
            return 0
        lax.fori_loop(0, PX, one, 0)

    @pl.when(gx == 0)
    def _():
        clear_planes(0)

    @pl.when(gx == NXD - 1)
    def _():
        clear_planes(13)

    @pl.when(gy == 0)
    def _():
        clear_rows(0)

    @pl.when(gy == NYD - 1)
    def _():
        clear_rows(40)

    starts = [4, 12, 20, 28, 36]
    ylow = (gy * 32 + sub - 4) >= 0
    yhigh = (gy * 32 + sub + 28) < 512

    def weights(p, _):
        place = gx * 8 + p - 5
        scale = jnp.where((place >= 0) & (place < 64), DAMP, 0.0).astype(F32)
        for r in starts:
            for t in range(3):
                w = scale / (1.05 + 240.0 * GC[1, p, t, pl.ds(r, 8), :])
                if r == 4:
                    w = jnp.where(ylow, w, 0.0)
                if r == 36:
                    w = jnp.where(yhigh, w, 0.0)
                if t == 2:
                    w = jnp.where(zmask, w, 0.0)
                W[p, t, pl.ds(r, 8), :] = w
        return 0

    lax.fori_loop(1, 17, weights, 0)

    def fine_sweep(src, dst, low, high, src_index=None):
        view = src if src_index is None else src.at[src_index]

        def one(p, _):
            for r in starts:
                for t, (v, s, b) in enumerate(stencil(view, p, r, 3, (0, 1, 2), True, lane, 1.0)):
                    rows = pl.ds(r, 8)
                    dst[p, t, rows, :] = 0.4 * v + W[p, t, rows, :] * (
                        GC[0, p, t, rows, :] + GC[1, p, t, rows, :] * s + b
                    )
            return 0

        lax.fori_loop(low, high, one, 0)

    def fine_residue(src, p):
        out = []
        for r in (8, 16, 24, 32):
            for t, (v, s, b) in enumerate(stencil(src, p, r, 3, (0, 1), True, lane, 1.0)):
                rows = pl.ds(r, 8)
                out.append(
                    GC[0, p, t, rows, :] - 1.05 * v + GC[1, p, t, rows, :] * (s - 240.0 * v) + b
                )
        return out

    fine_sweep(GC, A, 1, 17, 0)
    fine_sweep(A, B, 2, 16)

    def residue_pair(i, _):
        one = fine_residue(B, 5 + 2 * i)
        two = fine_residue(B, 6 + 2 * i)
        for n in range(8):
            RX[i, n % 2, pl.ds(8 * (n // 2), 8), :] = one[n] + two[n]
        return 0

    lax.fori_loop(0, 4, residue_pair, 0)
    coarsen_rows(0)

    for i in range(NC):
        coarse_copy(0, i).start()

    for i in range(NC):
        coarse_copy(1, i, True).wait_recv()
    for i in range(NC):
        coarse_copy(0, i, True).wait_recv()

    cylow = [(gy * 16 + sub + (r - 8)) >= 0 for r in (0, 24)]
    cyhigh = [(gy * 16 + sub + (r - 8)) < 256 for r in (0, 24)]

    def coarse_weights(p, _):
        place = gx * 4 + p - 5
        scale = jnp.where((place >= 0) & (place < 32), DAMP, 0.0).astype(F32)
        for n, r in enumerate((0, 8, 16, 24)):
            for t in range(2):
                w = scale / (1.05 + 60.0 * CO[1, p, t, pl.ds(r, 8), :])
                if r == 0:
                    w = jnp.where(cylow[0], w, 0.0)
                if r == 24:
                    w = jnp.where(cyhigh[1], w, 0.0)
                CW[p, t, pl.ds(r, 8), :] = w
                CA[p, t, pl.ds(r, 8), :] = w * CO[0, p, t, pl.ds(r, 8), :]
        return 0

    lax.fori_loop(0, CX, coarse_weights, 0)

    def coarse_sweep(src, dst, low, high):
        def one(p, _):
            for r in (4, 12, 20):
                for t, (v, s, b) in enumerate(stencil(src, p, r, 2, (0, 1), False, lane, 2.0)):
                    rows = pl.ds(r, 8)
                    dst[p, t, rows, :] = 0.4 * v + CW[p, t, rows, :] * (
                        CO[0, p, t, rows, :] + CO[1, p, t, rows, :] * s + b
                    )
            return 0

        lax.fori_loop(low, high, one, 0)

    coarse_sweep(CA, CB, 1, 13)
    coarse_sweep(CB, CA, 2, 12)
    coarse_sweep(CA, CB, 3, 11)

    ri = lax.broadcasted_iota(jnp.int32, (128, 256), 0)
    ci = lax.broadcasted_iota(jnp.int32, (128, 256), 1)
    spread = jnp.where(ci // 2 == ri, 1.0, 0.0).astype(F32)
    rh = lax.broadcasted_iota(jnp.int32, (128, 128), 0)
    ch = lax.broadcasted_iota(jnp.int32, (128, 128), 1)
    source = ch // 2 + 64 * gz
    keep = (ch >= zfirst) & (ch < zfirst + 8)
    spread_h = jnp.where((source == rh) & keep, 1.0, 0.0).astype(F32)
    mine = jnp.concatenate([CB[3 + q, gz, pl.ds(4, 24), :] for q in range(8)], axis=0)
    other = jnp.concatenate([CB[3 + q, 1 - gz, pl.ds(4, 24), :] for q in range(8)], axis=0)
    fine = jnp.dot(mine, spread, preferred_element_type=F32, precision=lax.Precision.HIGHEST)
    fine_h = jnp.dot(other, spread_h, preferred_element_type=F32, precision=lax.Precision.HIGHEST)
    for q in range(8):
        for t in range(3):
            part = (fine[24 * q : 24 * q + 24, 128 * t : 128 * t + 128] if t < 2
                    else fine_h[24 * q : 24 * q + 24])
            UPS[q, t, pl.ds(0, 24, stride=2), :] = part
            UPS[q, t, pl.ds(1, 24, stride=2), :] = part

    def add_up(q, _):
        for half in range(2):
            for r in range(6):
                for t in range(3):
                    rows = pl.ds(8 * r, 8)
                    p = 2 * q + 1 + half
                    A[p, t, rows, :] = B[p, t, rows, :] + UPS[q, t, rows, :]
        return 0

    lax.fori_loop(0, 8, add_up, 0)

    fine_sweep(A, B, 3, 15)
    fine_sweep(B, A, 4, 14)

    def finish(x, _):
        vals = fine_residue(A, 5 + x)
        for n in range(8):
            OUT[1, x, n % 2, pl.ds(8 * (n // 2), 8), :] = vals[n]
        for t in range(2):
            OUT[0, x, t] = A[5 + x, t, pl.ds(8, 32), :]
        return 0

    lax.fori_loop(0, 8, finish, 0)
    stores = []
    for a, dst in ((0, sol_hbm), (1, res_hbm)):
        for t in range(2):
            cp = pltpu.make_async_copy(
                OUT.at[a, :, t], dst.at[:, :, pl.ds(128 * t, 128)], out_sem.at[2 * a + t]
            )
            cp.start()
            stores.append(cp)

    for i in range(NM):
        main_copy(i).wait_send()
    for i in range(NP):
        pack_copy(i).wait_send()
    for k in range(2):
        for i in range(NC):
            coarse_copy(k, i).wait_send()
    for cp in stores:
        cp.wait()


def on_device(right_side, volscale):
    shape = jax.ShapeDtypeStruct(right_side.shape, F32)
    fine = pltpu.VMEM((PX, 3, ROWS, 128), F32)
    coarse = pltpu.VMEM((CX, 2, CROWS, 128), F32)
    any_space = pl.BlockSpec(memory_space=pl.ANY)
    return pl.pallas_call(
        kernel,
        out_shape=(shape, shape),
        in_specs=[any_space] * 2,
        out_specs=(any_space, any_space),
        scratch_shapes=[
            pltpu.VMEM((2, PX, 3, ROWS, 128), F32),
            pltpu.VMEM((8, 8, 128), F32),
            pltpu.VMEM((3, PX, 8, 128), F32),
            fine,
            fine,
            fine,
            pltpu.VMEM((4, 2, 32, 128), F32),
            pltpu.VMEM((2, CX, 2, CROWS, 128), F32),
            coarse,
            coarse,
            coarse,
            pltpu.VMEM((8, 3, ROWS, 128), F32),
            pltpu.VMEM((2, 8, 2, 32, 128), F32),
            pltpu.SemaphoreType.DMA((4,)),
            pltpu.SemaphoreType.DMA((NM,)),
            pltpu.SemaphoreType.DMA((NM,)),
            pltpu.SemaphoreType.DMA((NP,)),
            pltpu.SemaphoreType.DMA((NP,)),
            pltpu.SemaphoreType.DMA((2 * NC,)),
            pltpu.SemaphoreType.DMA((2 * NC,)),
            pltpu.SemaphoreType.DMA((4,)),
        ],
        compiler_params=pltpu.CompilerParams(collective_id=0, has_side_effects=True),
    )(right_side, volscale)


def solution(mesh):
    placed = (P("gx", "gy", "gz"), P("gx", "gy", "gz"))
    return jax.shard_map(
        on_device,
        mesh=mesh,
        in_specs=placed,
        out_specs=(P("gx", "gy", "gz"), P("gx", "gy", "gz")),
        check_vma=False,
    )
```

time: 321 us -> 59 us (0.18)
  the two profiles are of different devices: /device:TPU:184 before, /device:TPU:1 now
where the time goes in v1:
time: 59 us; the launch traced here: 58.9 us
  Pallas kernels  55.8 us (95%)
  local copies, waits for them, and re-layouts  2.42 us (4%)
  between operations  0.65 us (1%)
    pallas_call x1, Pallas kernels, on_device(): pl.pallas_call(kernel, out_shape=(shape, shape), in_specs=[any_space] * 2...  55.8 us
    unnamed x4, local copies, waits for them, and re-layouts  2.42 us

profile of v1, /device:TPU:1, one launch (start us, length us, event | category | flops | bytes accessed | tf_op | source)
XLA Modules:
  0.0 58.9 jit_solution(5677839180886179859)
XLA Ops:
  0.6 55.8 %shard_map.41 = (f32[8,32,256]{2,1,0:T(8,128)}, f32[8,32,256]{2,1,0:T(8,128)}) custom-call(f32[8,32,256]{2,1,0:T(8,128)} %g_hbm.1, f32[8,32,256]{2,1,0:T(8,128)} %c_hbm.1), custom_call_target="tpu_custom_call" | custom-call | tf_op jit(solution)/shard_map/pallas_call | solution.py:477
  56.4 0.0 copy-start
  56.4 1.7 %copy.6 = f32[8,32,256]{2,1,0:T(8,128)} copy(f32[8,32,256]{2,1,0:T(8,128)} %get-tuple-element.4) | data formatting | bytes 524288
  58.2 0.0 copy-done
  58.2 0.7 %copy.7 = f32[8,32,256]{2,1,0:T(8,128)} copy(f32[8,32,256]{2,1,0:T(8,128)S(1)} %copy-done) | data formatting | bytes 524288
Async XLA Ops:
  56.4 1.7 %copy-start = (f32[8,32,256]{2,1,0:T(8,128)S(1)}, f32[8,32,256]{2,1,0:T(8,128)}, u32[]{:S(2)}) copy-start(f32[8,32,256]{2,1,0:T(8,128)} %get-tuple-element.5) | copy-start | bytes 786436

commit v2 on v1

--- a/solution.py
+++ b/solution.py
@@ -145,11 +145,28 @@
     gx, gy, gz = lax.axis_index("gx"), lax.axis_index("gy"), lax.axis_index("gz")
 
     def peer(dx, dy, dz):
-        return (
-            lax.rem(gx + (dx + NXD), NXD),
-            lax.rem(gy + (dy + NYD), NYD),
-            lax.rem(gz + dz, 2),
-        )
+        return (gx + dx, gy + dy, lax.rem(gz + dz, 2))
+
+    def inside(dx, dy):
+        tests = []
+        if dx > 0:
+            tests.append(gx < NXD - dx)
+        if dx < 0:
+            tests.append(gx >= -dx)
+        if dy > 0:
+            tests.append(gy < NYD - dy)
+        if dy < 0:
+            tests.append(gy >= -dy)
+        if not tests:
+            return None
+        return tests[0] if len(tests) == 1 else tests[0] & tests[1]
+
+    def guarded(dx, dy, act):
+        test = inside(dx, dy)
+        if test is None:
+            act()
+        else:
+            pl.when(test)(act)
 
     loads = []
     for a, src in ((0, g_hbm), (1, c_hbm)):
@@ -163,19 +180,94 @@
             loads.append(cp)
 
     barrier = pltpu.get_barrier_semaphore()
-    for dx, dy, dz, *_ in COARSE:
-        pl.semaphore_signal(barrier, inc=1, device_id=peer(dx, dy, dz), device_id_type=MESH)
-
-    for cp in loads:
-        cp.wait()
+    partners = 0
+    for dx in (2, 1, 0, -1, -2):
+        for dy in (1, 0, -1):
+
+            def greet():
+                for dz in (0, 1):
+                    if (dx, dy, dz) != (0, 0, 0):
+                        pl.semaphore_signal(
+                            barrier, inc=1, device_id=peer(dx, dy, dz), device_id_type=MESH
+                        )
+
+            guarded(dx, dy, greet)
+            test = inside(dx, dy)
+            if test is None:
+                partners = partners + 1
+            else:
+                partners = partners + jnp.where(test, 2, 0)
 
     lane = lax.broadcasted_iota(jnp.int32, (8, 128), 1)
     sub = lax.broadcasted_iota(jnp.int32, (8, 128), 0)
     zfirst = 120 * gz
     zmask = (lane >= zfirst) & (lane < zfirst + 8)
+    blank = jnp.zeros((8, 128), F32)
+
+    def clear_fine(low, high, rows):
+        def one(p, _):
+            for a in range(2):
+                for t in range(2):
+                    for r in rows:
+                        GC[a, p, t, pl.ds(r, 8), :] = blank
+            return 0
+        lax.fori_loop(low, high, one, 0)
+
+    def clear_pack(slots, low, high):
+        def one(p, _):
+            for n in slots:
+                PR[n, p] = blank
+            return 0
+        lax.fori_loop(low, high, one, 0)
+
+    def clear_coarse(low, high, rows):
+        def one(p, _):
+            for k in range(2):
+                for t in range(2):
+                    for r in rows:
+                        CO[k, p, t, pl.ds(r, 8), :] = blank
+            return 0
+        lax.fori_loop(low, high, one, 0)
+
+    all_rows = (0, 8, 16, 24, 32, 40)
+
+    @pl.when(gx == 0)
+    def _():
+        clear_fine(0, 5, all_rows)
+        clear_pack((0, 1, 2), 0, 5)
+        clear_coarse(0, 5, (0, 8, 16, 24))
+
+    @pl.when(gx == 1)
+    def _():
+        clear_coarse(0, 1, (0, 8, 16, 24))
+
+    @pl.when(gx == NXD - 1)
+    def _():
+        clear_fine(13, 18, all_rows)
+        clear_pack((0, 1, 2), 13, 18)
+        clear_coarse(9, 14, (0, 8, 16, 24))
+
+    @pl.when(gx == NXD - 2)
+    def _():
+        clear_coarse(13, 14, (0, 8, 16, 24))
+
+    @pl.when(gy == 0)
+    def _():
+        clear_fine(0, 18, (0,))
+        clear_pack((0,), 0, 18)
+        clear_coarse(0, 14, (0,))
+
+    @pl.when(gy == NYD - 1)
+    def _():
+        clear_fine(0, 18, (40,))
+        clear_pack((2,), 0, 18)
+        clear_coarse(0, 14, (24,))
+
+    for cp in loads:
+        cp.wait()
 
     def pack_plane(x, _):
-        acc = jnp.zeros((8, 128), F32)
+        acc = blank
         for a in range(2):
             for j in range(4):
                 m = 4 * a + j
@@ -212,7 +304,9 @@
     lax.fori_loop(0, 4, pair_scale, 0)
     coarsen_rows(1)
 
-    pl.semaphore_wait(barrier, NC)
+    starts = [4, 12, 20, 28, 36]
+    ylow = (gy * 32 + sub - 4) >= 0
+    yhigh = (gy * 32 + sub + 28) < 512
 
     def main_copy(i):
         _, dx, dy, a, ps, pd, rs, rd = MAIN[i]
@@ -248,98 +342,115 @@
             device_id_type=MESH,
         )
 
-    early = [i for i in range(NM) if MAIN[i][0] == 0]
-    late = [i for i in range(NM) if MAIN[i][0] == 1]
-    for i in range(NP):
-        pack_copy(i).start()
-    for i in early:
-        main_copy(i).start()
-    for i in late:
-        main_copy(i).start()
-    for i in range(NC):
-        coarse_copy(1, i).start()
-
-    for i in range(NP):
-        pack_copy(i).wait_recv()
-    for i in early:
-        main_copy(i).wait_recv()
-    for i in late:
-        main_copy(i).wait_recv()
-
-    def unpack_plane(p, _):
-        for a in range(2):
-            for r in range(6):
-                slot, j = (0, 3) if r == 0 else (2, 0) if r == 5 else (1, r - 1)
-                m = 4 * a + j
-                v = pltpu.roll(PR[slot, p], (128 - 16 * m - 8) % 128, 1)
-                GC[a, p, 2, pl.ds(8 * r, 8), :] = jnp.where(zmask, v, 0.0)
-        return 0
-
-    lax.fori_loop(0, PX, unpack_plane, 0)
-
-    def clear_planes(first):
+    def fine_group(dx, dy, late):
+        copies = [main_copy(i) for i in range(NM)
+                  if MAIN[i][1:3] == (dx, dy) and MAIN[i][0] == late]
+        if not late:
+            copies = [pack_copy(i) for i in range(NP) if PACK[i][:2] == (dx, dy)] + copies
+        return copies
+
+    def coarse_group(k, dx, dy, arriving=False):
+        return [coarse_copy(k, i, arriving) for i in range(NC) if COARSE[i][:2] == (dx, dy)]
+
+    CORNERS = [(1, 1), (1, -1), (-1, 1), (-1, -1)]
+    SIDES = [(1, 0), (-1, 0)]
+    ROWSIDES = [(0, 1), (0, -1), (0, 0)]
+    FAR = [(2, 1), (2, -1), (-2, 1), (-2, -1)] + CORNERS + [(2, 0), (-2, 0)] + SIDES + ROWSIDES
+
+    def send(dx, dy, make):
+        def act():
+            for cp in make(dx, dy):
+                cp.start()
+        guarded(dx, dy, act)
+
+    def receive(dx, dy, make):
+        def act():
+            for cp in make(dx, dy):
+                cp.wait_recv()
+        guarded(-dx, -dy, act)
+
+    def sent(dx, dy, make):
+        def act():
+            for cp in make(dx, dy):
+                cp.wait_send()
+        guarded(dx, dy, act)
+
+    def early_copies(dx, dy):
+        return fine_group(dx, dy, 0)
+
+    def late_copies(dx, dy):
+        return fine_group(dx, dy, 1)
+
+    def scale_copies(dx, dy):
+        return coarse_group(1, dx, dy)
+
+    def rhs_copies(dx, dy):
+        return coarse_group(0, dx, dy)
+
+    pl.semaphore_wait(barrier, partners)
+
+    for d in CORNERS + ROWSIDES + SIDES:
+        send(*d, early_copies)
+    for d in CORNERS + SIDES:
+        send(*d, late_copies)
+    for d in FAR:
+        send(*d, scale_copies)
+
+    def unpack(low, high):
+        def unpack_plane(p, _):
+            for a in range(2):
+                for r in range(6):
+                    slot, j = (0, 3) if r == 0 else (2, 0) if r == 5 else (1, r - 1)
+                    m = 4 * a + j
+                    v = pltpu.roll(PR[slot, p], (128 - 16 * m - 8) % 128, 1)
+                    GC[a, p, 2, pl.ds(8 * r, 8), :] = jnp.where(zmask, v, 0.0)
+            return 0
+
+        lax.fori_loop(low, high, unpack_plane, 0)
+
+    def weights(low, high):
         def one(p, _):
-            GC[0, p] = jnp.zeros((3, ROWS, 128), F32)
-            return 0
-        lax.fori_loop(first, first + 5, one, 0)
-
-    def clear_rows(first):
-        def one(p, _):
-            for t in range(3):
-                GC[0, p, t, pl.ds(first, 8), :] = jnp.zeros((8, 128), F32)
-            return 0
-        lax.fori_loop(0, PX, one, 0)
-
-    @pl.when(gx == 0)
-    def _():
-        clear_planes(0)
-
-    @pl.when(gx == NXD - 1)
-    def _():
-        clear_planes(13)
-
-    @pl.when(gy == 0)
-    def _():
-        clear_rows(0)
-
-    @pl.when(gy == NYD - 1)
-    def _():
-        clear_rows(40)
-
-    starts = [4, 12, 20, 28, 36]
-    ylow = (gy * 32 + sub - 4) >= 0
-    yhigh = (gy * 32 + sub + 28) < 512
-
-    def weights(p, _):
-        place = gx * 8 + p - 5
-        scale = jnp.where((place >= 0) & (place < 64), DAMP, 0.0).astype(F32)
+            place = gx * 8 + p - 5
+            scale = jnp.where((place >= 0) & (place < 64), DAMP, 0.0).astype(F32)
+            for r in starts:
+                for t in range(3):
+                    w = scale / (1.05 + 240.0 * GC[1, p, t, pl.ds(r, 8), :])
+                    if r == 4:
+                        w = jnp.where(ylow, w, 0.0)
+                    if r == 36:
+                        w = jnp.where(yhigh, w, 0.0)
+                    if t == 2:
+                        w = jnp.where(zmask, w, 0.0)
+                    W[p, t, pl.ds(r, 8), :] = w
+            return 0
+
+        lax.fori_loop(low, high, one, 0)
+
+    def fine_plane(view, dst, p):
         for r in starts:
-            for t in range(3):
-                w = scale / (1.05 + 240.0 * GC[1, p, t, pl.ds(r, 8), :])
-                if r == 4:
-                    w = jnp.where(ylow, w, 0.0)
-                if r == 36:
-                    w = jnp.where(yhigh, w, 0.0)
-                if t == 2:
-                    w = jnp.where(zmask, w, 0.0)
-                W[p, t, pl.ds(r, 8), :] = w
-        return 0
-
-    lax.fori_loop(1, 17, weights, 0)
+            for t, (v, s, b) in enumerate(stencil(view, p, r, 3, (0, 1, 2), True, lane, 1.0)):
+                rows = pl.ds(r, 8)
+                dst[p, t, rows, :] = 0.4 * v + W[p, t, rows, :] * (
+                    GC[0, p, t, rows, :] + GC[1, p, t, rows, :] * s + b
+                )
 
     def fine_sweep(src, dst, low, high, src_index=None):
         view = src if src_index is None else src.at[src_index]
 
         def one(p, _):
-            for r in starts:
-                for t, (v, s, b) in enumerate(stencil(view, p, r, 3, (0, 1, 2), True, lane, 1.0)):
-                    rows = pl.ds(r, 8)
-                    dst[p, t, rows, :] = 0.4 * v + W[p, t, rows, :] * (
-                        GC[0, p, t, rows, :] + GC[1, p, t, rows, :] * s + b
-                    )
+            fine_plane(view, dst, p)
             return 0
 
         lax.fori_loop(low, high, one, 0)
+
+    def fine_sides(src, dst, low, high, count, src_index=None):
+        view = src if src_index is None else src.at[src_index]
+
+        def one(n, _):
+            fine_plane(view, dst, jnp.where(n < count, low + n, high + n - count))
+            return 0
+
+        lax.fori_loop(0, 2 * count, one, 0)
 
     def fine_residue(src, p):
         out = []
@@ -351,8 +462,20 @@
                 )
         return out
 
-    fine_sweep(GC, A, 1, 17, 0)
-    fine_sweep(A, B, 2, 16)
+    for d in ROWSIDES:
+        receive(*d, early_copies)
+    unpack(5, 13)
+    weights(5, 13)
+    fine_sweep(GC, A, 6, 12, 0)
+    fine_sweep(A, B, 7, 11)
+    for d in CORNERS + SIDES:
+        receive(*d, early_copies)
+    unpack(2, 5)
+    unpack(13, 16)
+    weights(3, 5)
+    weights(13, 15)
+    fine_sides(GC, A, 3, 12, 3, 0)
+    fine_sides(A, B, 4, 11, 3)
 
     def residue_pair(i, _):
         one = fine_residue(B, 5 + 2 * i)
@@ -364,16 +487,23 @@
     lax.fori_loop(0, 4, residue_pair, 0)
     coarsen_rows(0)
 
-    for i in range(NC):
-        coarse_copy(0, i).start()
-
-    for i in range(NC):
-        coarse_copy(1, i, True).wait_recv()
-    for i in range(NC):
-        coarse_copy(0, i, True).wait_recv()
-
-    cylow = [(gy * 16 + sub + (r - 8)) >= 0 for r in (0, 24)]
-    cyhigh = [(gy * 16 + sub + (r - 8)) < 256 for r in (0, 24)]
+    for d in FAR:
+        send(*d, rhs_copies)
+
+    for d in CORNERS + SIDES:
+        receive(*d, late_copies)
+    unpack(0, 2)
+    unpack(16, 18)
+    weights(1, 3)
+    weights(15, 17)
+    fine_sides(GC, A, 1, 15, 2, 0)
+    fine_sides(A, B, 2, 14, 2)
+
+    cylow = (gy * 16 + sub - 8) >= 0
+    cyhigh = (gy * 16 + sub + 16) < 256
+
+    for d in FAR:
+        receive(*d, lambda dx, dy: coarse_group(1, dx, dy, True))
 
     def coarse_weights(p, _):
         place = gx * 4 + p - 5
@@ -382,14 +512,25 @@
             for t in range(2):
                 w = scale / (1.05 + 60.0 * CO[1, p, t, pl.ds(r, 8), :])
                 if r == 0:
-                    w = jnp.where(cylow[0], w, 0.0)
+                    w = jnp.where(cylow, w, 0.0)
                 if r == 24:
-                    w = jnp.where(cyhigh[1], w, 0.0)
+                    w = jnp.where(cyhigh, w, 0.0)
                 CW[p, t, pl.ds(r, 8), :] = w
-                CA[p, t, pl.ds(r, 8), :] = w * CO[0, p, t, pl.ds(r, 8), :]
         return 0
 
     lax.fori_loop(0, CX, coarse_weights, 0)
+
+    for d in FAR:
+        receive(*d, lambda dx, dy: coarse_group(0, dx, dy, True))
+
+    def coarse_first(p, _):
+        for r in (0, 8, 16, 24):
+            for t in range(2):
+                rows = pl.ds(r, 8)
+                CA[p, t, rows, :] = CW[p, t, rows, :] * CO[0, p, t, rows, :]
+        return 0
+
+    lax.fori_loop(0, CX, coarse_first, 0)
 
     def coarse_sweep(src, dst, low, high):
         def one(p, _):
@@ -440,31 +581,33 @@
     fine_sweep(A, B, 3, 15)
     fine_sweep(B, A, 4, 14)
 
+    stores = []
+
+    def store(a, dst):
+        for t in range(2):
+            src = OUT.at[:, t] if a else A.at[pl.ds(5, 8), t, pl.ds(8, 32), :]
+            cp = pltpu.make_async_copy(src, dst.at[:, :, pl.ds(128 * t, 128)], out_sem.at[2 * a + t])
+            cp.start()
+            stores.append(cp)
+
+    store(0, sol_hbm)
+
     def finish(x, _):
         vals = fine_residue(A, 5 + x)
         for n in range(8):
-            OUT[1, x, n % 2, pl.ds(8 * (n // 2), 8), :] = vals[n]
-        for t in range(2):
-            OUT[0, x, t] = A[5 + x, t, pl.ds(8, 32), :]
+            OUT[x, n % 2, pl.ds(8 * (n // 2), 8), :] = vals[n]
         return 0
 
     lax.fori_loop(0, 8, finish, 0)
-    stores = []
-    for a, dst in ((0, sol_hbm), (1, res_hbm)):
-        for t in range(2):
-            cp = pltpu.make_async_copy(
-                OUT.at[a, :, t], dst.at[:, :, pl.ds(128 * t, 128)], out_sem.at[2 * a + t]
-            )
-            cp.start()
-            stores.append(cp)
-
-    for i in range(NM):
-        main_copy(i).wait_send()
-    for i in range(NP):
-        pack_copy(i).wait_send()
-    for k in range(2):
-        for i in range(NC):
-            coarse_copy(k, i).wait_send()
+    store(1, res_hbm)
+
+    for d in CORNERS + ROWSIDES + SIDES:
+        sent(*d, early_copies)
+    for d in CORNERS + SIDES:
+        sent(*d, late_copies)
+    for d in FAR:
+        sent(*d, scale_copies)
+        sent(*d, rhs_copies)
     for cp in stores:
         cp.wait()
 
@@ -492,7 +635,7 @@
             coarse,
             coarse,
             pltpu.VMEM((8, 3, ROWS, 128), F32),
-            pltpu.VMEM((2, 8, 2, 32, 128), F32),
+            pltpu.VMEM((8, 2, 32, 128), F32),
             pltpu.SemaphoreType.DMA((4,)),
             pltpu.SemaphoreType.DMA((NM,)),
             pltpu.SemaphoreType.DMA((NM,)),

time: 59 us -> 49.4 us (0.84)
  the two profiles are of different devices: /device:TPU:1 before, /device:TPU:25 now
where the time goes in v2:
time: 49.4 us; the launch traced here: 49.3 us
  Pallas kernels  46.3 us (94%)
  local copies, waits for them, and re-layouts  2.42 us (5%)
  between operations  0.65 us (1%)
    pallas_call x1, Pallas kernels, on_device(): pl.pallas_call(kernel, out_shape=(shape, shape), in_specs=[any_space] * 2...  46.3 us
    unnamed x4, local copies, waits for them, and re-layouts  2.42 us

profile of v2, /device:TPU:25, one launch (start us, length us, event | category | flops | bytes accessed | tf_op | source)
XLA Modules:
  0.0 49.3 jit_solution(5219067223999902708)
XLA Ops:
  0.6 46.3 %shard_map.41 = (f32[8,32,256]{2,1,0:T(8,128)}, f32[8,32,256]{2,1,0:T(8,128)}) custom-call(f32[8,32,256]{2,1,0:T(8,128)} %g_hbm.1, f32[8,32,256]{2,1,0:T(8,128)} %c_hbm.1), custom_call_target="tpu_custom_call" | custom-call | tf_op jit(solution)/shard_map/pallas_call | solution.py:620
  46.9 0.0 copy-start
  46.9 1.7 %copy.6 = f32[8,32,256]{2,1,0:T(8,128)} copy(f32[8,32,256]{2,1,0:T(8,128)} %get-tuple-element.4) | data formatting | bytes 524288
  48.6 0.0 copy-done
  48.6 0.7 %copy.7 = f32[8,32,256]{2,1,0:T(8,128)} copy(f32[8,32,256]{2,1,0:T(8,128)S(1)} %copy-done) | data formatting | bytes 524288
Async XLA Ops:
  46.9 1.7 %copy-start = (f32[8,32,256]{2,1,0:T(8,128)S(1)}, f32[8,32,256]{2,1,0:T(8,128)}, u32[]{:S(2)}) copy-start(f32[8,32,256]{2,1,0:T(8,128)} %get-tuple-element.5) | copy-start | bytes 786436

commit v3 on v2

--- a/solution.py
+++ b/solution.py
@@ -17,67 +17,52 @@
 DAMP = 0.6
 
 
-def main_messages():
-    out = []
-    for dx in (1, -1, 0):
-        for dy in (0, 1, -1):
-            if dx == 0 and dy == 0:
-                continue
-            if dy == 0:
-                rs, rd = (8, 32), (8, 32)
-            elif dy == 1:
-                rs, rd = (35, 5), (3, 5)
-            else:
-                rs, rd = (8, 5), (40, 5)
-            if dx == 0:
-                for a in (0, 1):
-                    out.append((0, dx, dy, a, (5, 8), (5, 8), rs, rd))
-            elif dx == 1:
-                out.append((0, dx, dy, 0, (10, 3), (2, 3), rs, rd))
-                out.append((0, dx, dy, 1, (11, 2), (3, 2), rs, rd))
-                out.append((1, dx, dy, 0, (8, 2), (0, 2), rs, rd))
-                out.append((1, dx, dy, 1, (9, 2), (1, 2), rs, rd))
-            else:
-                out.append((0, dx, dy, 0, (5, 3), (13, 3), rs, rd))
-                out.append((0, dx, dy, 1, (5, 2), (13, 2), rs, rd))
-                out.append((1, dx, dy, 0, (8, 2), (16, 2), rs, rd))
-                out.append((1, dx, dy, 1, (7, 2), (15, 2), rs, rd))
-    return out
-
-
-def pack_messages():
-    out = []
-    for dx in (1, -1, 0):
-        for dy in (0, 1, -1):
-            ps, pd = {0: ((0, 8), (5, 8)), 1: ((3, 5), (0, 5)), -1: ((0, 5), (13, 5))}[dx]
-            rs = {0: (0, 8), 1: (3, 5), -1: (0, 5)}[dy]
-            out.append((dx, dy, ps, pd, rs))
+def fine_messages():
+    out = [("z", 0, 0, 1, ("PS",), ("PR", 1, (5, 8), (0, 8)))]
+    lo, mid, hi = (3, 5), (8, 32), (40, 5)
+    for dx in (1, -1):
+        sg, dg = ((10, 3), (2, 3)) if dx == 1 else ((5, 3), (13, 3))
+        sc, dc = ((11, 2), (3, 2)) if dx == 1 else ((5, 2), (13, 2))
+        out.append(("x", dx, 0, 0, ("GC", 0, sg, mid), ("GC", 0, dg, mid)))
+        out.append(("x", dx, 0, 0, ("GC", 1, sc, mid), ("GC", 1, dc, mid)))
+        for rows in (lo, hi):
+            out.append(("xc", dx, 0, 0, ("GC", 0, sg, rows), ("GC", 0, dg, rows)))
+            out.append(("xc", dx, 0, 0, ("GC", 1, sc, rows), ("GC", 1, dc, rows)))
+        out.append(("xc", dx, 0, 0, ("PA", sg), ("PA", dg)))
+        sg, dg = ((8, 2), (0, 2)) if dx == 1 else ((8, 2), (16, 2))
+        sc, dc = ((9, 2), (1, 2)) if dx == 1 else ((7, 2), (15, 2))
+        out.append(("xl", dx, 0, 0, ("GC", 0, sg, (3, 42)), ("GC", 0, dg, (3, 42))))
+        out.append(("xl", dx, 0, 0, ("GC", 1, sc, (3, 42)), ("GC", 1, dc, (3, 42))))
+        out.append(("xl", dx, 0, 0, ("PA", sg), ("PA", dg)))
+    for dy in (1, -1):
+        rs, rd, pr = ((35, 5), lo, (3, 5)) if dy == 1 else ((8, 5), hi, (0, 5))
+        out.append(("y", 0, dy, 0, ("GC", 0, (5, 8), rs), ("GC", 0, (5, 8), rd)))
+        out.append(("y", 0, dy, 0, ("GC", 1, (5, 8), rs), ("GC", 1, (5, 8), rd)))
+        out.append(("yz", 0, dy, 0, ("PR", 1, (5, 8), pr), ("PR", 1 - dy, (5, 8), pr)))
     return out
 
 
 def coarse_messages():
     out = []
-    for dz in (0, 1):
-        for dx in (1, -1, 2, -2, 0):
-            for dy in (0, 1, -1):
-                if dx == 0 and dy == 0 and dz == 0:
-                    continue
-                ps, pd = {
-                    0: ((5, 4), (5, 4)),
-                    1: ((5, 4), (1, 4)),
-                    -1: ((5, 4), (9, 4)),
-                    2: ((8, 1), (0, 1)),
-                    -2: ((5, 1), (13, 1)),
-                }[dx]
-                rs, rd = {0: ((8, 16), (8, 16)), 1: ((19, 5), (3, 5)), -1: ((8, 5), (24, 5))}[dy]
-                out.append((dx, dy, dz, ps, pd, rs, rd))
+    for dx in (2, 1, 0, -1, -2):
+        for dy in (1, 0, -1):
+            ps, pd = {
+                0: ((5, 4), (5, 4)),
+                1: ((5, 4), (1, 4)),
+                -1: ((5, 4), (9, 4)),
+                2: ((8, 1), (0, 1)),
+                -2: ((5, 1), (13, 1)),
+            }[dx]
+            rs, rd = {0: ((8, 16), (8, 16)), 1: ((19, 5), (3, 5)), -1: ((8, 5), (24, 5))}[dy]
+            if (dx, dy) != (0, 0):
+                out.append((dx, dy, 0, ps, pd, rs, rd))
+            out.append((dx, dy, 1, None, None, {0: (0, 8), 1: (3, 5), -1: (0, 5)}[dy], None))
     return out
 
 
-MAIN = main_messages()
-PACK = pack_messages()
+FINE = fine_messages()
 COARSE = coarse_messages()
-NM, NP, NC = len(MAIN), len(PACK), len(COARSE)
+NF, NC = len(FINE), len(COARSE)
 
 
 def ds(pair):
@@ -140,8 +125,8 @@
     return result
 
 
-def kernel(g_hbm, c_hbm, sol_hbm, res_hbm, GC, PS, PR, W, A, B, RX, CO, CW, CA, CB, UPS, OUT,
-           load_sem, m_send, m_recv, p_send, p_recv, c_send, c_recv, out_sem):
+def kernel(g_hbm, c_hbm, sol_hbm, res_hbm, GC, PS, PR, W, A, B, RX, CO, QS, QR, CW, CA, CB, UPS,
+           OUT, load_sem, f_send, f_recv, c_send, c_recv, out_sem):
     gx, gy, gz = lax.axis_index("gx"), lax.axis_index("gy"), lax.axis_index("gz")
 
     def peer(dx, dy, dz):
@@ -180,23 +165,15 @@
             loads.append(cp)
 
     barrier = pltpu.get_barrier_semaphore()
-    partners = 0
-    for dx in (2, 1, 0, -1, -2):
-        for dy in (1, 0, -1):
-
-            def greet():
-                for dz in (0, 1):
-                    if (dx, dy, dz) != (0, 0, 0):
-                        pl.semaphore_signal(
-                            barrier, inc=1, device_id=peer(dx, dy, dz), device_id_type=MESH
-                        )
-
-            guarded(dx, dy, greet)
-            test = inside(dx, dy)
-            if test is None:
-                partners = partners + 1
-            else:
-                partners = partners + jnp.where(test, 2, 0)
+    partners = 1
+    for dx, dy, dz in ((1, 0, 0), (-1, 0, 0), (0, 1, 0), (0, -1, 0), (0, 0, 1)):
+
+        def greet():
+            pl.semaphore_signal(barrier, inc=1, device_id=peer(dx, dy, dz), device_id_type=MESH)
+
+        guarded(dx, dy, greet)
+        if not dz:
+            partners = partners + jnp.where(inside(dx, dy), 1, 0)
 
     lane = lax.broadcasted_iota(jnp.int32, (8, 128), 1)
     sub = lax.broadcasted_iota(jnp.int32, (8, 128), 0)
@@ -223,45 +200,56 @@
     def clear_coarse(low, high, rows):
         def one(p, _):
             for k in range(2):
-                for t in range(2):
-                    for r in rows:
-                        CO[k, p, t, pl.ds(r, 8), :] = blank
+                for r in rows:
+                    CO[k, p, 0, pl.ds(r, 8), :] = blank
             return 0
         lax.fori_loop(low, high, one, 0)
 
     all_rows = (0, 8, 16, 24, 32, 40)
+
+    def clear_edge(cols, rows):
+        for k in range(2):
+            for n in cols:
+                for m in rows:
+                    QR[k, n, m] = blank
 
     @pl.when(gx == 0)
     def _():
         clear_fine(0, 5, all_rows)
         clear_pack((0, 1, 2), 0, 5)
         clear_coarse(0, 5, (0, 8, 16, 24))
+        clear_edge((0, 1), (0, 1, 2))
 
     @pl.when(gx == 1)
     def _():
         clear_coarse(0, 1, (0, 8, 16, 24))
+        clear_edge((0,), (0, 1, 2))
 
     @pl.when(gx == NXD - 1)
     def _():
         clear_fine(13, 18, all_rows)
         clear_pack((0, 1, 2), 13, 18)
         clear_coarse(9, 14, (0, 8, 16, 24))
+        clear_edge((3, 4), (0, 1, 2))
 
     @pl.when(gx == NXD - 2)
     def _():
         clear_coarse(13, 14, (0, 8, 16, 24))
+        clear_edge((4,), (0, 1, 2))
 
     @pl.when(gy == 0)
     def _():
-        clear_fine(0, 18, (0,))
-        clear_pack((0,), 0, 18)
+        clear_fine(5, 13, (0,))
+        clear_pack((0,), 5, 13)
         clear_coarse(0, 14, (0,))
+        clear_edge((0, 1, 2, 3, 4), (0,))
 
     @pl.when(gy == NYD - 1)
     def _():
-        clear_fine(0, 18, (40,))
-        clear_pack((2,), 0, 18)
+        clear_fine(5, 13, (40,))
+        clear_pack((2,), 5, 13)
         clear_coarse(0, 14, (24,))
+        clear_edge((0, 1, 2, 3, 4), (2,))
 
     for cp in loads:
         cp.wait()
@@ -293,8 +281,14 @@
             pieces.append(jnp.concatenate(cols, axis=1))
         allp = jnp.concatenate(pieces, axis=0)
         q = jnp.dot(allp, pool, preferred_element_type=F32, precision=lax.Precision.HIGHEST)
+        acc = blank
         for i in range(4):
-            CO[k, 5 + i, gz, pl.ds(8, 16), :] = q[16 * i : 16 * i + 16]
+            CO[k, 5 + i, 0, pl.ds(8, 16), :] = q[16 * i : 16 * i + 16]
+            for j in range(2):
+                m = 2 * i + j
+                turned = pltpu.roll(q[8 * m : 8 * m + 8], (16 * m + 8) % 128, 1)
+                acc = jnp.where((lane >= 16 * m) & (lane < 16 * m + 16), turned, acc)
+        QS[k] = acc
 
     def pair_scale(i, _):
         for t in range(2):
@@ -308,93 +302,67 @@
     ylow = (gy * 32 + sub - 4) >= 0
     yhigh = (gy * 32 + sub + 28) < 512
 
-    def main_copy(i):
-        _, dx, dy, a, ps, pd, rs, rd = MAIN[i]
+    def place(where):
+        if where[0] == "PS":
+            return PS
+        if where[0] == "PR":
+            return PR.at[where[1], ds(where[2]), ds(where[3]), :]
+        if where[0] == "PA":
+            return PR.at[:, ds(where[1])]
+        return GC.at[where[1], ds(where[2]), pl.ds(0, 2), ds(where[3]), :]
+
+    def fine_copy(i):
+        _, dx, dy, dz, src, dst = FINE[i]
         return pltpu.make_async_remote_copy(
-            src_ref=GC.at[a, ds(ps), pl.ds(0, 2), ds(rs), :],
-            dst_ref=GC.at[a, ds(pd), pl.ds(0, 2), ds(rd), :],
-            send_sem=m_send.at[i],
-            recv_sem=m_recv.at[i],
-            device_id=peer(dx, dy, 0),
+            src_ref=place(src),
+            dst_ref=place(dst),
+            send_sem=f_send.at[i],
+            recv_sem=f_recv.at[i],
+            device_id=peer(dx, dy, dz),
             device_id_type=MESH,
         )
 
-    def pack_copy(i):
-        dx, dy, ps, pd, rs = PACK[i]
+    def coarse_copy(k, i):
+        dx, dy, dz, ps, pd, rs, rd = COARSE[i]
+        if dz:
+            src, dst = QS.at[k, ds(rs), :], QR.at[k, 2 - dx, 1 - dy, ds(rs), :]
+        else:
+            src, dst = CO.at[k, ds(ps), 0, ds(rs), :], CO.at[k, ds(pd), 0, ds(rd), :]
         return pltpu.make_async_remote_copy(
-            src_ref=PS.at[ds(ps), ds(rs), :],
-            dst_ref=PR.at[1 - dy, ds(pd), ds(rs), :],
-            send_sem=p_send.at[i],
-            recv_sem=p_recv.at[i],
-            device_id=peer(dx, dy, 1),
-            device_id_type=MESH,
-        )
-
-    def coarse_copy(k, i, arriving=False):
-        dx, dy, dz, ps, pd, rs, rd = COARSE[i]
-        tile = lax.rem(gz + dz, 2) if arriving else gz
-        return pltpu.make_async_remote_copy(
-            src_ref=CO.at[k, ds(ps), tile, ds(rs), :],
-            dst_ref=CO.at[k, ds(pd), tile, ds(rd), :],
+            src_ref=src,
+            dst_ref=dst,
             send_sem=c_send.at[k * NC + i],
             recv_sem=c_recv.at[k * NC + i],
             device_id=peer(dx, dy, dz),
             device_id_type=MESH,
         )
 
-    def fine_group(dx, dy, late):
-        copies = [main_copy(i) for i in range(NM)
-                  if MAIN[i][1:3] == (dx, dy) and MAIN[i][0] == late]
-        if not late:
-            copies = [pack_copy(i) for i in range(NP) if PACK[i][:2] == (dx, dy)] + copies
-        return copies
-
-    def coarse_group(k, dx, dy, arriving=False):
-        return [coarse_copy(k, i, arriving) for i in range(NC) if COARSE[i][:2] == (dx, dy)]
-
-    CORNERS = [(1, 1), (1, -1), (-1, 1), (-1, -1)]
-    SIDES = [(1, 0), (-1, 0)]
-    ROWSIDES = [(0, 1), (0, -1), (0, 0)]
-    FAR = [(2, 1), (2, -1), (-2, 1), (-2, -1)] + CORNERS + [(2, 0), (-2, 0)] + SIDES + ROWSIDES
-
-    def send(dx, dy, make):
-        def act():
-            for cp in make(dx, dy):
-                cp.start()
-        guarded(dx, dy, act)
-
-    def receive(dx, dy, make):
-        def act():
-            for cp in make(dx, dy):
-                cp.wait_recv()
-        guarded(-dx, -dy, act)
-
-    def sent(dx, dy, make):
-        def act():
-            for cp in make(dx, dy):
-                cp.wait_send()
-        guarded(dx, dy, act)
-
-    def early_copies(dx, dy):
-        return fine_group(dx, dy, 0)
-
-    def late_copies(dx, dy):
-        return fine_group(dx, dy, 1)
-
-    def scale_copies(dx, dy):
-        return coarse_group(1, dx, dy)
-
-    def rhs_copies(dx, dy):
-        return coarse_group(0, dx, dy)
+    FAR = [(2, 1), (2, -1), (-2, 1), (-2, -1), (1, 1), (1, -1), (-1, 1), (-1, -1),
+           (2, 0), (-2, 0), (1, 0), (-1, 0), (0, 1), (0, -1), (0, 0)]
+    NEAR = [(1, 0), (-1, 0), (0, 1), (0, -1), (0, 0)]
+
+    def run(direction, copies, method, back):
+        if copies:
+            dx, dy = direction
+            def act():
+                for cp in copies:
+                    getattr(cp, method)()
+            guarded(-dx if back else dx, -dy if back else dy, act)
+
+    def fine(phase, method):
+        for d in NEAR:
+            run(d, [fine_copy(i) for i in range(NF) if FINE[i][0] in phase and FINE[i][1:3] == d],
+                method, method == "wait_recv")
+
+    def coarse(k, method):
+        for d in FAR:
+            run(d, [coarse_copy(k, i) for i in range(NC) if COARSE[i][:2] == d],
+                method, method == "wait_recv")
 
     pl.semaphore_wait(barrier, partners)
 
-    for d in CORNERS + ROWSIDES + SIDES:
-        send(*d, early_copies)
-    for d in CORNERS + SIDES:
-        send(*d, late_copies)
-    for d in FAR:
-        send(*d, scale_copies)
+    fine(("z",), "start")
+    fine(("x", "y"), "start")
 
     def unpack(low, high):
         def unpack_plane(p, _):
@@ -410,8 +378,8 @@
 
     def weights(low, high):
         def one(p, _):
-            place = gx * 8 + p - 5
-            scale = jnp.where((place >= 0) & (place < 64), DAMP, 0.0).astype(F32)
+            at = gx * 8 + p - 5
+            scale = jnp.where((at >= 0) & (at < 64), DAMP, 0.0).astype(F32)
             for r in starts:
                 for t in range(3):
                     w = scale / (1.05 + 240.0 * GC[1, p, t, pl.ds(r, 8), :])
@@ -462,14 +430,17 @@
                 )
         return out
 
-    for d in ROWSIDES:
-        receive(*d, early_copies)
+    fine(("z",), "wait_recv")
+    fine(("yz",), "start")
+    fine(("y", "yz"), "wait_recv")
+    fine(("xc",), "start")
+    fine(("xl",), "start")
     unpack(5, 13)
     weights(5, 13)
     fine_sweep(GC, A, 6, 12, 0)
     fine_sweep(A, B, 7, 11)
-    for d in CORNERS + SIDES:
-        receive(*d, early_copies)
+    fine(("x", "xc"), "wait_recv")
+    coarse(1, "start")
     unpack(2, 5)
     unpack(13, 16)
     weights(3, 5)
@@ -487,11 +458,9 @@
     lax.fori_loop(0, 4, residue_pair, 0)
     coarsen_rows(0)
 
-    for d in FAR:
-        send(*d, rhs_copies)
-
-    for d in CORNERS + SIDES:
-        receive(*d, late_copies)
+    coarse(0, "start")
+
+    fine(("xl",), "wait_recv")
     unpack(0, 2)
     unpack(16, 18)
     weights(1, 3)
@@ -502,12 +471,22 @@
     cylow = (gy * 16 + sub - 8) >= 0
     cyhigh = (gy * 16 + sub + 16) < 256
 
-    for d in FAR:
-        receive(*d, lambda dx, dy: coarse_group(1, dx, dy, True))
+    coarse(1, "wait_recv")
+
+    def coarse_unpack(k):
+        for p in range(CX):
+            col, i = [(0, 3), (1, 0), (1, 1), (1, 2), (1, 3), (2, 0), (2, 1), (2, 2), (2, 3),
+                      (3, 0), (3, 1), (3, 2), (3, 3), (4, 0)][p]
+            for r, (row, j) in enumerate(((0, 1), (1, 0), (1, 1), (2, 0))):
+                m = 2 * i + j
+                turned = pltpu.roll(QR[k, col, row], (128 - 16 * m - 8) % 128, 1)
+                CO[k, p, 1, pl.ds(8 * r, 8), :] = jnp.where(zmask, turned, 0.0)
+
+    coarse_unpack(1)
 
     def coarse_weights(p, _):
-        place = gx * 4 + p - 5
-        scale = jnp.where((place >= 0) & (place < 32), DAMP, 0.0).astype(F32)
+        at = gx * 4 + p - 5
+        scale = jnp.where((at >= 0) & (at < 32), DAMP, 0.0).astype(F32)
         for n, r in enumerate((0, 8, 16, 24)):
             for t in range(2):
                 w = scale / (1.05 + 60.0 * CO[1, p, t, pl.ds(r, 8), :])
@@ -515,13 +494,15 @@
                     w = jnp.where(cylow, w, 0.0)
                 if r == 24:
                     w = jnp.where(cyhigh, w, 0.0)
+                if t == 1:
+                    w = jnp.where(zmask, w, 0.0)
                 CW[p, t, pl.ds(r, 8), :] = w
         return 0
 
     lax.fori_loop(0, CX, coarse_weights, 0)
 
-    for d in FAR:
-        receive(*d, lambda dx, dy: coarse_group(0, dx, dy, True))
+    coarse(0, "wait_recv")
+    coarse_unpack(0)
 
     def coarse_first(p, _):
         for r in (0, 8, 16, 24):
@@ -535,7 +516,7 @@
     def coarse_sweep(src, dst, low, high):
         def one(p, _):
             for r in (4, 12, 20):
-                for t, (v, s, b) in enumerate(stencil(src, p, r, 2, (0, 1), False, lane, 2.0)):
+                for t, (v, s, b) in enumerate(stencil(src, p, r, 2, (0, 1), True, lane, 2.0)):
                     rows = pl.ds(r, 8)
                     dst[p, t, rows, :] = 0.4 * v + CW[p, t, rows, :] * (
                         CO[0, p, t, rows, :] + CO[1, p, t, rows, :] * s + b
@@ -556,14 +537,14 @@
     source = ch // 2 + 64 * gz
     keep = (ch >= zfirst) & (ch < zfirst + 8)
     spread_h = jnp.where((source == rh) & keep, 1.0, 0.0).astype(F32)
-    mine = jnp.concatenate([CB[3 + q, gz, pl.ds(4, 24), :] for q in range(8)], axis=0)
-    other = jnp.concatenate([CB[3 + q, 1 - gz, pl.ds(4, 24), :] for q in range(8)], axis=0)
-    fine = jnp.dot(mine, spread, preferred_element_type=F32, precision=lax.Precision.HIGHEST)
-    fine_h = jnp.dot(other, spread_h, preferred_element_type=F32, precision=lax.Precision.HIGHEST)
+    mine = jnp.concatenate([CB[3 + q, 0, pl.ds(4, 24), :] for q in range(8)], axis=0)
+    other = jnp.concatenate([CB[3 + q, 1, pl.ds(4, 24), :] for q in range(8)], axis=0)
+    wide = jnp.dot(mine, spread, preferred_element_type=F32, precision=lax.Precision.HIGHEST)
+    wide_h = jnp.dot(other, spread_h, preferred_element_type=F32, precision=lax.Precision.HIGHEST)
     for q in range(8):
         for t in range(3):
-            part = (fine[24 * q : 24 * q + 24, 128 * t : 128 * t + 128] if t < 2
-                    else fine_h[24 * q : 24 * q + 24])
+            part = (wide[24 * q : 24 * q + 24, 128 * t : 128 * t + 128] if t < 2
+                    else wide_h[24 * q : 24 * q + 24])
             UPS[q, t, pl.ds(0, 24, stride=2), :] = part
             UPS[q, t, pl.ds(1, 24, stride=2), :] = part
 
@@ -601,13 +582,9 @@
     lax.fori_loop(0, 8, finish, 0)
     store(1, res_hbm)
 
-    for d in CORNERS + ROWSIDES + SIDES:
-        sent(*d, early_copies)
-    for d in CORNERS + SIDES:
-        sent(*d, late_copies)
-    for d in FAR:
-        sent(*d, scale_copies)
-        sent(*d, rhs_copies)
+    fine(("z", "x", "y", "yz", "xc", "xl"), "wait_send")
+    coarse(1, "wait_send")
+    coarse(0, "wait_send")
     for cp in stores:
         cp.wait()
 
@@ -631,16 +608,16 @@
             fine,
             pltpu.VMEM((4, 2, 32, 128), F32),
             pltpu.VMEM((2, CX, 2, CROWS, 128), F32),
+            pltpu.VMEM((2, 8, 128), F32),
+            pltpu.VMEM((2, 5, 3, 8, 128), F32),
             coarse,
             coarse,
             coarse,
             pltpu.VMEM((8, 3, ROWS, 128), F32),
             pltpu.VMEM((8, 2, 32, 128), F32),
             pltpu.SemaphoreType.DMA((4,)),
-            pltpu.SemaphoreType.DMA((NM,)),
-            pltpu.SemaphoreType.DMA((NM,)),
-            pltpu.SemaphoreType.DMA((NP,)),
-            pltpu.SemaphoreType.DMA((NP,)),
+            pltpu.SemaphoreType.DMA((NF,)),
+            pltpu.SemaphoreType.DMA((NF,)),
             pltpu.SemaphoreType.DMA((2 * NC,)),
             pltpu.SemaphoreType.DMA((2 * NC,)),
             pltpu.SemaphoreType.DMA((4,)),

time: 49.4 us -> 43.4 us (0.88)
  the two profiles are of different devices: /device:TPU:25 before, /device:TPU:89 now
where the time goes in v3:
time: 43.4 us; the launch traced here: 43.2 us
  Pallas kernels  40.2 us (93%)
  local copies, waits for them, and re-layouts  2.42 us (6%)
  between operations  0.65 us (1%)
    pallas_call x1, Pallas kernels, on_device(): pl.pallas_call(kernel, out_shape=(shape, shape), in_specs=[any_space] * 2...  40.2 us
    unnamed x4, local copies, waits for them, and re-layouts  2.42 us

profile of v3, /device:TPU:89, one launch (start us, length us, event | category | flops | bytes accessed | tf_op | source)
XLA Modules:
  0.0 43.2 jit_solution(17441650289787806169)
XLA Ops:
  0.6 40.2 %shard_map.41 = (f32[8,32,256]{2,1,0:T(8,128)}, f32[8,32,256]{2,1,0:T(8,128)}) custom-call(f32[8,32,256]{2,1,0:T(8,128)} %g_hbm.1, f32[8,32,256]{2,1,0:T(8,128)} %c_hbm.1), custom_call_target="tpu_custom_call" | custom-call | tf_op jit(solution)/shard_map/pallas_call | solution.py:597
  40.8 0.0 copy-start
  40.8 1.7 %copy.6 = f32[8,32,256]{2,1,0:T(8,128)} copy(f32[8,32,256]{2,1,0:T(8,128)} %get-tuple-element.4) | data formatting | bytes 524288
  42.5 0.0 copy-done
  42.5 0.7 %copy.7 = f32[8,32,256]{2,1,0:T(8,128)} copy(f32[8,32,256]{2,1,0:T(8,128)S(1)} %copy-done) | data formatting | bytes 524288
Async XLA Ops:
  40.8 1.7 %copy-start = (f32[8,32,256]{2,1,0:T(8,128)S(1)}, f32[8,32,256]{2,1,0:T(8,128)}, u32[]{:S(2)}) copy-start(f32[8,32,256]{2,1,0:T(8,128)} %get-tuple-element.5) | copy-start | bytes 786436

commit v4 on v3

--- a/solution.py
+++ b/solution.py
@@ -77,56 +77,54 @@
     return pltpu.roll(x, 1, 1)
 
 
-def shifts(vals, lane, circular):
-    count = len(vals)
-    ups = [up(v) for v in vals]
-    downs = [down(v) for v in vals]
-    zero = jnp.zeros_like(vals[0])
-    plus, minus = [], []
-    for t in range(count):
-        nxt = ups[(t + 1) % count] if circular or t + 1 < count else zero
-        prv = downs[t - 1] if circular or t > 0 else zero
-        plus.append(jnp.where(lane == 127, nxt, ups[t]))
-        minus.append(jnp.where(lane == 0, prv, downs[t]))
-    return plus, minus
-
-
-def stencil(ref, p, r, tiles, outs, circular, lane, h):
+def stencil(ref, before, after, p, r, tiles, outs, lane, h):
     sf = 1.0 / (h * h)
     bf = 1.0 / h
-    centre, parts, mixed = [], [], []
+    rows = pl.ds(r, 8)
+    centre, straight, drift, plus, minus = [], [], [], [], []
     for t in range(tiles):
-        v = ref[p, t, pl.ds(r, 8), :]
-        xm = ref[p - 1, t, pl.ds(r, 8), :]
-        xp = ref[p + 1, t, pl.ds(r, 8), :]
+        v = ref[p, t, rows, :]
+        xm = ref[p - 1, t, rows, :]
+        xp = ref[p + 1, t, rows, :]
         ym = ref[p, t, pl.ds(r - 1, 8), :]
         yp = ref[p, t, pl.ds(r + 1, 8), :]
         d = xp - xm
         fy = yp - ym
+        flat = (32.0 * sf) * v
+        mixed = (1.5 * sf) * (d - fy)
+        slope = (0.75 * bf) * v
+        plus.append(before[p, t, rows, :] * (flat + mixed) + slope)
+        minus.append(after[p, t, rows, :] * (flat - mixed) - slope)
         centre.append(v)
-        mixed.append(d - fy)
         if t in outs:
             dyy = (ref[p + 1, t, pl.ds(r + 1, 8), :] - ref[p - 1, t, pl.ds(r + 1, 8), :]) - (
                 ref[p + 1, t, pl.ds(r - 1, 8), :] - ref[p - 1, t, pl.ds(r - 1, 8), :]
             )
-            s = (48.0 * sf) * (xp + xm) + (40.0 * sf) * (yp + ym) + (2.0 * sf) * dyy
-            b = (1.5 * bf) * d - bf * fy
+            straight.append((48.0 * sf) * (xp + xm) + (40.0 * sf) * (yp + ym) + (2.0 * sf) * dyy)
+            drift.append((1.5 * bf) * d - bf * fy)
         else:
-            s = b = None
-        parts.append((s, b))
-    vp, vm = shifts(centre, lane, circular)
-    hp, hm = shifts(mixed, lane, circular)
+            straight.append(None)
+            drift.append(None)
     result = []
     for t in outs:
-        s, b = parts[t]
-        s = s + (32.0 * sf) * (vp[t] + vm[t]) + (1.5 * sf) * (hp[t] - hm[t])
-        b = b + (0.75 * bf) * (vp[t] - vm[t])
-        result.append((centre[t], s, b))
+        b = (
+            drift[t]
+            + up(jnp.where(lane == 0, plus[(t + 1) % tiles], plus[t]))
+            + down(jnp.where(lane == 127, minus[t - 1], minus[t]))
+        )
+        result.append((centre[t], straight[t], b))
     return result
 
 
-def kernel(g_hbm, c_hbm, sol_hbm, res_hbm, GC, PS, PR, W, A, B, RX, CO, QS, QR, CW, CA, CB, UPS,
-           OUT, load_sem, f_send, f_recv, c_send, c_recv, out_sem):
+def shifted_scales(values, lane):
+    count = len(values)
+    before = [down(jnp.where(lane == 127, values[t - 1], values[t])) for t in range(count)]
+    after = [up(jnp.where(lane == 0, values[(t + 1) % count], values[t])) for t in range(count)]
+    return before, after
+
+
+def kernel(g_hbm, c_hbm, sol_ref, res_ref, GC, PS, PR, W, FB, FA, A, B, RX, CO, QS, QR,
+           CW, KB, KA, CA, CB, UPS, load_sem, f_send, f_recv, c_send, c_recv):
     gx, gy, gz = lax.axis_index("gx"), lax.axis_index("gy"), lax.axis_index("gz")
 
     def peer(dx, dy, dz):
@@ -381,8 +379,12 @@
             at = gx * 8 + p - 5
             scale = jnp.where((at >= 0) & (at < 64), DAMP, 0.0).astype(F32)
             for r in starts:
+                scales = [GC[1, p, t, pl.ds(r, 8), :] for t in range(3)]
+                before, after = shifted_scales(scales, lane)
                 for t in range(3):
-                    w = scale / (1.05 + 240.0 * GC[1, p, t, pl.ds(r, 8), :])
+                    FB[p, t, pl.ds(r, 8), :] = before[t]
+                    FA[p, t, pl.ds(r, 8), :] = after[t]
+                    w = scale / (1.05 + 240.0 * scales[t])
                     if r == 4:
                         w = jnp.where(ylow, w, 0.0)
                     if r == 36:
@@ -396,7 +398,7 @@
 
     def fine_plane(view, dst, p):
         for r in starts:
-            for t, (v, s, b) in enumerate(stencil(view, p, r, 3, (0, 1, 2), True, lane, 1.0)):
+            for t, (v, s, b) in enumerate(stencil(view, FB, FA, p, r, 3, (0, 1, 2), lane, 1.0)):
                 rows = pl.ds(r, 8)
                 dst[p, t, rows, :] = 0.4 * v + W[p, t, rows, :] * (
                     GC[0, p, t, rows, :] + GC[1, p, t, rows, :] * s + b
@@ -405,25 +407,27 @@
     def fine_sweep(src, dst, low, high, src_index=None):
         view = src if src_index is None else src.at[src_index]
 
-        def one(p, _):
-            fine_plane(view, dst, p)
-            return 0
-
-        lax.fori_loop(low, high, one, 0)
+        def one(n, _):
+            fine_plane(view, dst, low + 2 * n)
+            fine_plane(view, dst, low + 2 * n + 1)
+            return 0
+
+        lax.fori_loop(0, (high - low) // 2, one, 0)
 
     def fine_sides(src, dst, low, high, count, src_index=None):
         view = src if src_index is None else src.at[src_index]
 
         def one(n, _):
-            fine_plane(view, dst, jnp.where(n < count, low + n, high + n - count))
-            return 0
-
-        lax.fori_loop(0, 2 * count, one, 0)
+            fine_plane(view, dst, low + n)
+            fine_plane(view, dst, high + n)
+            return 0
+
+        lax.fori_loop(0, count, one, 0)
 
     def fine_residue(src, p):
         out = []
         for r in (8, 16, 24, 32):
-            for t, (v, s, b) in enumerate(stencil(src, p, r, 3, (0, 1), True, lane, 1.0)):
+            for t, (v, s, b) in enumerate(stencil(src, FB, FA, p, r, 3, (0, 1), lane, 1.0)):
                 rows = pl.ds(r, 8)
                 out.append(
                     GC[0, p, t, rows, :] - 1.05 * v + GC[1, p, t, rows, :] * (s - 240.0 * v) + b
@@ -488,8 +492,12 @@
         at = gx * 4 + p - 5
         scale = jnp.where((at >= 0) & (at < 32), DAMP, 0.0).astype(F32)
         for n, r in enumerate((0, 8, 16, 24)):
+            scales = [CO[1, p, t, pl.ds(r, 8), :] for t in range(2)]
+            before, after = shifted_scales(scales, lane)
             for t in range(2):
-                w = scale / (1.05 + 60.0 * CO[1, p, t, pl.ds(r, 8), :])
+                KB[p, t, pl.ds(r, 8), :] = before[t]
+                KA[p, t, pl.ds(r, 8), :] = after[t]
+                w = scale / (1.05 + 60.0 * scales[t])
                 if r == 0:
                     w = jnp.where(cylow, w, 0.0)
                 if r == 24:
@@ -514,16 +522,20 @@
     lax.fori_loop(0, CX, coarse_first, 0)
 
     def coarse_sweep(src, dst, low, high):
-        def one(p, _):
-            for r in (4, 12, 20):
-                for t, (v, s, b) in enumerate(stencil(src, p, r, 2, (0, 1), True, lane, 2.0)):
-                    rows = pl.ds(r, 8)
-                    dst[p, t, rows, :] = 0.4 * v + CW[p, t, rows, :] * (
-                        CO[0, p, t, rows, :] + CO[1, p, t, rows, :] * s + b
-                    )
-            return 0
-
-        lax.fori_loop(low, high, one, 0)
+        def one(n, _):
+            for half in range(2):
+                p = low + 2 * n + half
+                for r in (4, 12, 20):
+                    for t, (v, s, b) in enumerate(
+                        stencil(src, KB, KA, p, r, 2, (0, 1), lane, 2.0)
+                    ):
+                        rows = pl.ds(r, 8)
+                        dst[p, t, rows, :] = 0.4 * v + CW[p, t, rows, :] * (
+                            CO[0, p, t, rows, :] + CO[1, p, t, rows, :] * s + b
+                        )
+            return 0
+
+        lax.fori_loop(0, (high - low) // 2, one, 0)
 
     coarse_sweep(CA, CB, 1, 13)
     coarse_sweep(CB, CA, 2, 12)
@@ -562,35 +574,23 @@
     fine_sweep(A, B, 3, 15)
     fine_sweep(B, A, 4, 14)
 
-    stores = []
-
-    def store(a, dst):
-        for t in range(2):
-            src = OUT.at[:, t] if a else A.at[pl.ds(5, 8), t, pl.ds(8, 32), :]
-            cp = pltpu.make_async_copy(src, dst.at[:, :, pl.ds(128 * t, 128)], out_sem.at[2 * a + t])
-            cp.start()
-            stores.append(cp)
-
-    store(0, sol_hbm)
-
     def finish(x, _):
         vals = fine_residue(A, 5 + x)
         for n in range(8):
-            OUT[x, n % 2, pl.ds(8 * (n // 2), 8), :] = vals[n]
+            t, r = n % 2, 8 * (n // 2)
+            res_ref[x, pl.ds(r, 8), pl.ds(128 * t, 128)] = vals[n]
+            sol_ref[x, pl.ds(r, 8), pl.ds(128 * t, 128)] = A[5 + x, t, pl.ds(8 + r, 8), :]
         return 0
 
     lax.fori_loop(0, 8, finish, 0)
-    store(1, res_hbm)
 
     fine(("z", "x", "y", "yz", "xc", "xl"), "wait_send")
     coarse(1, "wait_send")
     coarse(0, "wait_send")
-    for cp in stores:
-        cp.wait()
 
 
 def on_device(right_side, volscale):
-    shape = jax.ShapeDtypeStruct(right_side.shape, F32)
+    shape = pltpu.VMEM(right_side.shape, F32)
     fine = pltpu.VMEM((PX, 3, ROWS, 128), F32)
     coarse = pltpu.VMEM((CX, 2, CROWS, 128), F32)
     any_space = pl.BlockSpec(memory_space=pl.ANY)
@@ -598,11 +598,13 @@
         kernel,
         out_shape=(shape, shape),
         in_specs=[any_space] * 2,
-        out_specs=(any_space, any_space),
+        out_specs=(pl.BlockSpec(memory_space=pltpu.VMEM),) * 2,
         scratch_shapes=[
             pltpu.VMEM((2, PX, 3, ROWS, 128), F32),
             pltpu.VMEM((8, 8, 128), F32),
             pltpu.VMEM((3, PX, 8, 128), F32),
+            fine,
+            fine,
             fine,
             fine,
             fine,
@@ -613,14 +615,14 @@
             coarse,
             coarse,
             coarse,
+            coarse,
+            coarse,
             pltpu.VMEM((8, 3, ROWS, 128), F32),
-            pltpu.VMEM((8, 2, 32, 128), F32),
             pltpu.SemaphoreType.DMA((4,)),
             pltpu.SemaphoreType.DMA((NF,)),
             pltpu.SemaphoreType.DMA((NF,)),
             pltpu.SemaphoreType.DMA((2 * NC,)),
             pltpu.SemaphoreType.DMA((2 * NC,)),
-            pltpu.SemaphoreType.DMA((4,)),
         ],
         compiler_params=pltpu.CompilerParams(collective_id=0, has_side_effects=True),
     )(right_side, volscale)

time: 43.4 us -> 38.9 us (0.90)
  Pallas kernels: 40.2 us -> 36.8 us
  local copies, waits for them, and re-layouts: 2.42 us -> 1.41 us
    pallas_call x1, Pallas kernels: 40.2 us -> 36.8 us  [on_device(): pl.pallas_call(kernel, out_shape=(shape, shape), in_specs=[any_space] * 2...]
    unnamed x4 -> x2, local copies, waits for them, and re-layouts: 2.42 us -> 1.41 us
where the time goes in v4:
time: 38.9 us; the launch traced here: 38.8 us
  Pallas kernels  36.8 us (95%)
  local copies, waits for them, and re-layouts  1.41 us (4%)
  between operations  0.64 us (2%)
    pallas_call x1, Pallas kernels, on_device(): pl.pallas_call(kernel, out_shape=(shape, shape), in_specs=[any_space] * 2...  36.8 us
    unnamed x2, local copies, waits for them, and re-layouts  1.41 us

profile of v4, /device:TPU:89, one launch (start us, length us, event | category | flops | bytes accessed | tf_op | source)
XLA Modules:
  0.0 38.8 jit_solution(13069969301441665052)
XLA Ops:
  0.6 36.8 %shard_map.41 = (f32[8,32,256]{2,1,0:T(8,128)S(1)}, f32[8,32,256]{2,1,0:T(8,128)S(1)}) custom-call(f32[8,32,256]{2,1,0:T(8,128)} %g_hbm.1, f32[8,32,256]{2,1,0:T(8,128)} %c_hbm.1), custom_call_target="tpu_custom_call" | custom-call | tf_op jit(solution)/shard_map/pallas_call | solution.py:597
  37.4 0.7 %copy.6 = f32[8,32,256]{2,1,0:T(8,128)} copy(f32[8,32,256]{2,1,0:T(8,128)S(1)} %get-tuple-element.2) | data formatting | bytes 524288
  38.1 0.7 %copy.7 = f32[8,32,256]{2,1,0:T(8,128)} copy(f32[8,32,256]{2,1,0:T(8,128)S(1)} %get-tuple-element.3) | data formatting | bytes 524288

commit v5 on v4

--- a/solution.py
+++ b/solution.py
@@ -18,27 +18,40 @@
 
 
 def fine_messages():
-    out = [("z", 0, 0, 1, ("PS",), ("PR", 1, (5, 8), (0, 8)))]
     lo, mid, hi = (3, 5), (8, 32), (40, 5)
+    every = (0, 3)
+    out = [
+        ("z", 0, 0, 1, ("PS",), ("PR", (1, 1), (5, 8), (0, 8))),
+        ("z", 0, 0, 1, ("QS", 1), ("QR", 2, (1, 1), (0, 8))),
+    ]
     for dx in (1, -1):
+        side, far = 2 - dx, 2 - 2 * dx
         sg, dg = ((10, 3), (2, 3)) if dx == 1 else ((5, 3), (13, 3))
         sc, dc = ((11, 2), (3, 2)) if dx == 1 else ((5, 2), (13, 2))
         out.append(("x", dx, 0, 0, ("GC", 0, sg, mid), ("GC", 0, dg, mid)))
         out.append(("x", dx, 0, 0, ("GC", 1, sc, mid), ("GC", 1, dc, mid)))
+        out.append(("xz", dx, 0, 0, ("PR", (1, 1), sg, (0, 8)), ("PR", (1, 1), dg, (0, 8))))
         for rows in (lo, hi):
-            out.append(("xc", dx, 0, 0, ("GC", 0, sg, rows), ("GC", 0, dg, rows)))
-            out.append(("xc", dx, 0, 0, ("GC", 1, sc, rows), ("GC", 1, dc, rows)))
-        out.append(("xc", dx, 0, 0, ("PA", sg), ("PA", dg)))
-        sg, dg = ((8, 2), (0, 2)) if dx == 1 else ((8, 2), (16, 2))
-        sc, dc = ((9, 2), (1, 2)) if dx == 1 else ((7, 2), (15, 2))
-        out.append(("xl", dx, 0, 0, ("GC", 0, sg, (3, 42)), ("GC", 0, dg, (3, 42))))
-        out.append(("xl", dx, 0, 0, ("GC", 1, sc, (3, 42)), ("GC", 1, dc, (3, 42))))
-        out.append(("xl", dx, 0, 0, ("PA", sg), ("PA", dg)))
+            out.append(("xy", dx, 0, 0, ("GC", 0, sg, rows), ("GC", 0, dg, rows)))
+            out.append(("xy", dx, 0, 0, ("GC", 1, sc, rows), ("GC", 1, dc, rows)))
+        for slot, rows in ((0, (3, 5)), (2, (0, 5))):
+            out.append(("xyz", dx, 0, 0, ("PR", (slot, 1), sg, rows), ("PR", (slot, 1), dg, rows)))
+        out.append(("cx", dx, 0, 0, ("CO", (5, 4), (3, 26)), ("CO", (1 if dx == 1 else 9, 4), (3, 26))))
+        out.append(("cx", dx, 0, 0, ("QR", 2, every, (0, 8)), ("QR", side, every, (0, 8))))
+        near, last = (4, 0) if dx == 1 else (9, 13)
+        out.append(("cxx", dx, 0, 0, ("CO", (near, 1), (3, 26)), ("CO", (last, 1), (3, 26))))
+        out.append(("cxx", dx, 0, 0, ("QR", side, every, (0, 8)), ("QR", far, every, (0, 8))))
+        sb, db = ((10, 2), (2, 2)) if dx == 1 else ((6, 2), (14, 2))
+        out.append(("s", dx, 0, 0, ("B", sb), ("B", db)))
+        out.append(("s", dx, 0, 0, ("SS", (1 - dx) // 2), ("SR", (1 - dx) // 2)))
     for dy in (1, -1):
         rs, rd, pr = ((35, 5), lo, (3, 5)) if dy == 1 else ((8, 5), hi, (0, 5))
+        cs, cd = ((19, 5), (3, 5)) if dy == 1 else ((8, 5), (24, 5))
         out.append(("y", 0, dy, 0, ("GC", 0, (5, 8), rs), ("GC", 0, (5, 8), rd)))
         out.append(("y", 0, dy, 0, ("GC", 1, (5, 8), rs), ("GC", 1, (5, 8), rd)))
-        out.append(("yz", 0, dy, 0, ("PR", 1, (5, 8), pr), ("PR", 1 - dy, (5, 8), pr)))
+        out.append(("yz", 0, dy, 0, ("PR", (1, 1), (5, 8), pr), ("PR", (1 - dy, 1), (5, 8), pr)))
+        out.append(("cy", 0, dy, 0, ("CO", (5, 4), cs), ("CO", (5, 4), cd)))
+        out.append(("cy", 0, dy, 0, ("QR", 2, (1, 1), pr), ("QR", 2, (1 - dy, 1), pr)))
     return out
 
 
@@ -77,43 +90,66 @@
     return pltpu.roll(x, 1, 1)
 
 
-def stencil(ref, before, after, p, r, tiles, outs, lane, h):
-    sf = 1.0 / (h * h)
-    bf = 1.0 / h
+RATIO = 64.0 / 3.0
+
+
+def stencil(ref, factors, base, count, r, tiles, outs, lane, bf):
+    before, before_v, after, after_v = factors
     rows = pl.ds(r, 8)
-    centre, straight, drift, plus, minus = [], [], [], [], []
+    parts = []
+    for k in range(count):
+        parts.append(([], [], [], [], []))
     for t in range(tiles):
-        v = ref[p, t, rows, :]
-        xm = ref[p - 1, t, rows, :]
-        xp = ref[p + 1, t, rows, :]
-        ym = ref[p, t, pl.ds(r - 1, 8), :]
-        yp = ref[p, t, pl.ds(r + 1, 8), :]
-        d = xp - xm
-        fy = yp - ym
-        flat = (32.0 * sf) * v
-        mixed = (1.5 * sf) * (d - fy)
-        slope = (0.75 * bf) * v
-        plus.append(before[p, t, rows, :] * (flat + mixed) + slope)
-        minus.append(after[p, t, rows, :] * (flat - mixed) - slope)
-        centre.append(v)
-        if t in outs:
-            dyy = (ref[p + 1, t, pl.ds(r + 1, 8), :] - ref[p - 1, t, pl.ds(r + 1, 8), :]) - (
-                ref[p + 1, t, pl.ds(r - 1, 8), :] - ref[p - 1, t, pl.ds(r - 1, 8), :]
+        vs = [ref[base - 1 + k, t, rows, :] for k in range(count + 2)]
+        fys = []
+        for k in range(count + 2):
+            if t in outs or 0 < k <= count:
+                fys.append(
+                    ref[base - 1 + k, t, pl.ds(r + 1, 8), :]
+                    - ref[base - 1 + k, t, pl.ds(r - 1, 8), :]
+                )
+            else:
+                fys.append(None)
+        for k in range(count):
+            centre, straight, drift, plus, minus = parts[k]
+            p = base + k
+            v, xm, xp, fy = vs[k + 1], vs[k], vs[k + 2], fys[k + 1]
+            d = xp - xm
+            m = d - fy
+            plus.append(before_v[p, t, rows, :] * v + before[p, t, rows, :] * m)
+            minus.append(after_v[p, t, rows, :] * v - after[p, t, rows, :] * m)
+            centre.append(v)
+            if t in outs:
+                sy = ref[p, t, pl.ds(r + 1, 8), :] + ref[p, t, pl.ds(r - 1, 8), :]
+                straight.append(24.0 * (xp + xm) + 20.0 * sy + (fys[k + 2] - fys[k]))
+                drift.append((1.5 * bf) * d - (fy if bf == 1.0 else bf * fy))
+            else:
+                straight.append(None)
+                drift.append(None)
+    result = []
+    for k in range(count):
+        centre, straight, drift, plus, minus = parts[k]
+        one = []
+        for t in outs:
+            b = (
+                drift[t]
+                + up(jnp.where(lane == 0, plus[(t + 1) % tiles], plus[t]))
+                + down(jnp.where(lane == 127, minus[t - 1], minus[t]))
             )
-            straight.append((48.0 * sf) * (xp + xm) + (40.0 * sf) * (yp + ym) + (2.0 * sf) * dyy)
-            drift.append((1.5 * bf) * d - bf * fy)
-        else:
-            straight.append(None)
-            drift.append(None)
-    result = []
-    for t in outs:
-        b = (
-            drift[t]
-            + up(jnp.where(lane == 0, plus[(t + 1) % tiles], plus[t]))
-            + down(jnp.where(lane == 127, minus[t - 1], minus[t]))
-        )
-        result.append((centre[t], straight[t], b))
+            one.append((t, centre[t], straight[t], b))
+        result.append(one)
     return result
+
+
+def keep_factors(stores, p, rows, scales, lane, sf, bf):
+    double, before, before_v, after, after_v = stores
+    low, high = shifted_scales([(1.5 * sf) * c for c in scales], lane)
+    for t in range(len(scales)):
+        double[p, t, rows, :] = (2.0 * sf) * scales[t]
+        before[p, t, rows, :] = low[t]
+        before_v[p, t, rows, :] = RATIO * low[t] + 0.75 * bf
+        after[p, t, rows, :] = high[t]
+        after_v[p, t, rows, :] = RATIO * high[t] - 0.75 * bf
 
 
 def shifted_scales(values, lane):
@@ -123,8 +159,8 @@
     return before, after
 
 
-def kernel(g_hbm, c_hbm, sol_ref, res_ref, GC, PS, PR, W, FB, FA, A, B, RX, CO, QS, QR,
-           CW, KB, KA, CA, CB, UPS, load_sem, f_send, f_recv, c_send, c_recv):
+def kernel(g_hbm, c_hbm, sol_ref, res_ref, GC, PS, PR, SS, SR, W, F2, FB, FBV, FA, FAV, A, B, RX, CO, QS, QR,
+           CW, K2, KB, KBV, KA, KAV, CA, CB, UPS, load_sem, f_send, f_recv, c_send, c_recv):
     gx, gy, gz = lax.axis_index("gx"), lax.axis_index("gy"), lax.axis_index("gz")
 
     def peer(dx, dy, dz):
@@ -195,59 +231,73 @@
             return 0
         lax.fori_loop(low, high, one, 0)
 
-    def clear_coarse(low, high, rows):
+    def clear_coarse(k, low, high, rows):
         def one(p, _):
-            for k in range(2):
-                for r in rows:
-                    CO[k, p, 0, pl.ds(r, 8), :] = blank
+            for r in rows:
+                CO[k, p, 0, pl.ds(r, 8), :] = blank
             return 0
         lax.fori_loop(low, high, one, 0)
 
+    def clear_edge(k, cols, rows):
+        for n in cols:
+            for m in rows:
+                QR[k, n, m] = blank
+
+    def clear_smooth(low):
+        for p in (low, low + 1):
+            for t in range(3):
+                for r in (0, 8, 16, 24, 32, 40):
+                    B[p, t, pl.ds(r, 8), :] = blank
+
     all_rows = (0, 8, 16, 24, 32, 40)
-
-    def clear_edge(cols, rows):
-        for k in range(2):
-            for n in cols:
-                for m in rows:
-                    QR[k, n, m] = blank
+    coarse_rows = (0, 8, 16, 24)
+    slots = (0, 1, 2)
 
     @pl.when(gx == 0)
     def _():
-        clear_fine(0, 5, all_rows)
-        clear_pack((0, 1, 2), 0, 5)
-        clear_coarse(0, 5, (0, 8, 16, 24))
-        clear_edge((0, 1), (0, 1, 2))
+        clear_fine(2, 5, all_rows)
+        clear_pack(slots, 2, 5)
+        for k in range(2):
+            clear_coarse(k, 0, 5, coarse_rows)
+            clear_edge(k, (0, 1), slots)
+        clear_smooth(2)
 
     @pl.when(gx == 1)
     def _():
-        clear_coarse(0, 1, (0, 8, 16, 24))
-        clear_edge((0,), (0, 1, 2))
+        clear_coarse(0, 0, 1, coarse_rows)
+        clear_edge(0, (0,), slots)
 
     @pl.when(gx == NXD - 1)
     def _():
-        clear_fine(13, 18, all_rows)
-        clear_pack((0, 1, 2), 13, 18)
-        clear_coarse(9, 14, (0, 8, 16, 24))
-        clear_edge((3, 4), (0, 1, 2))
+        clear_fine(13, 16, all_rows)
+        clear_pack(slots, 13, 16)
+        for k in range(2):
+            clear_coarse(k, 9, 14, coarse_rows)
+            clear_edge(k, (3, 4), slots)
+        clear_smooth(14)
 
     @pl.when(gx == NXD - 2)
     def _():
-        clear_coarse(13, 14, (0, 8, 16, 24))
-        clear_edge((4,), (0, 1, 2))
+        clear_coarse(0, 13, 14, coarse_rows)
+        clear_edge(0, (4,), slots)
 
     @pl.when(gy == 0)
     def _():
         clear_fine(5, 13, (0,))
         clear_pack((0,), 5, 13)
-        clear_coarse(0, 14, (0,))
-        clear_edge((0, 1, 2, 3, 4), (0,))
+        clear_coarse(0, 0, 14, (0,))
+        clear_coarse(1, 5, 9, (0,))
+        clear_edge(0, (0, 1, 2, 3, 4), (0,))
+        clear_edge(1, (2,), (0,))
 
     @pl.when(gy == NYD - 1)
     def _():
         clear_fine(5, 13, (40,))
         clear_pack((2,), 5, 13)
-        clear_coarse(0, 14, (24,))
-        clear_edge((0, 1, 2, 3, 4), (2,))
+        clear_coarse(0, 0, 14, (24,))
+        clear_coarse(1, 5, 9, (24,))
+        clear_edge(0, (0, 1, 2, 3, 4), (2,))
+        clear_edge(1, (2,), (2,))
 
     for cp in loads:
         cp.wait()
@@ -301,12 +351,27 @@
     yhigh = (gy * 32 + sub + 28) < 512
 
     def place(where):
-        if where[0] == "PS":
-            return PS
-        if where[0] == "PR":
-            return PR.at[where[1], ds(where[2]), ds(where[3]), :]
-        if where[0] == "PA":
-            return PR.at[:, ds(where[1])]
+        kind = where[0]
+        if kind == "PS":
+            return PS.at[pl.ds(0, 8)]
+        if kind == "PR":
+            slot, planes, rows = where[1:]
+            return PR.at[slot[0], ds(planes), ds(rows), :]
+        if kind == "QS":
+            return QS.at[where[1]]
+        if kind == "QR":
+            col, rows, subs = where[1:]
+            if rows[1] == 1:
+                return QR.at[1, col, rows[0], ds(subs), :]
+            return QR.at[1, col, ds(rows), ds(subs), :]
+        if kind == "CO":
+            return CO.at[1, ds(where[1]), 0, ds(where[2]), :]
+        if kind == "B":
+            return B.at[ds(where[1]), pl.ds(0, 2), pl.ds(4, 40), :]
+        if kind == "SS":
+            return SS.at[where[1]]
+        if kind == "SR":
+            return SR.at[where[1]]
         return GC.at[where[1], ds(where[2]), pl.ds(0, 2), ds(where[3]), :]
 
     def fine_copy(i):
@@ -329,8 +394,8 @@
         return pltpu.make_async_remote_copy(
             src_ref=src,
             dst_ref=dst,
-            send_sem=c_send.at[k * NC + i],
-            recv_sem=c_recv.at[k * NC + i],
+            send_sem=c_send.at[i],
+            recv_sem=c_recv.at[i],
             device_id=peer(dx, dy, dz),
             device_id_type=MESH,
         )
@@ -360,7 +425,8 @@
     pl.semaphore_wait(barrier, partners)
 
     fine(("z",), "start")
-    fine(("x", "y"), "start")
+    fine(("y",), "start")
+    fine(("x",), "start")
 
     def unpack(low, high):
         def unpack_plane(p, _):
@@ -380,10 +446,8 @@
             scale = jnp.where((at >= 0) & (at < 64), DAMP, 0.0).astype(F32)
             for r in starts:
                 scales = [GC[1, p, t, pl.ds(r, 8), :] for t in range(3)]
-                before, after = shifted_scales(scales, lane)
+                keep_factors((F2, FB, FBV, FA, FAV), p, pl.ds(r, 8), scales, lane, 1.0, 1.0)
                 for t in range(3):
-                    FB[p, t, pl.ds(r, 8), :] = before[t]
-                    FA[p, t, pl.ds(r, 8), :] = after[t]
                     w = scale / (1.05 + 240.0 * scales[t])
                     if r == 4:
                         w = jnp.where(ylow, w, 0.0)
@@ -396,65 +460,75 @@
 
         lax.fori_loop(low, high, one, 0)
 
-    def fine_plane(view, dst, p):
+    fine_factors = (FB, FBV, FA, FAV)
+
+    def fine_planes(view, dst, base, count):
         for r in starts:
-            for t, (v, s, b) in enumerate(stencil(view, FB, FA, p, r, 3, (0, 1, 2), lane, 1.0)):
-                rows = pl.ds(r, 8)
-                dst[p, t, rows, :] = 0.4 * v + W[p, t, rows, :] * (
-                    GC[0, p, t, rows, :] + GC[1, p, t, rows, :] * s + b
-                )
-
-    def fine_sweep(src, dst, low, high, src_index=None):
+            rows = pl.ds(r, 8)
+            whole = stencil(view, fine_factors, base, count, r, 3, (0, 1, 2), lane, 1.0)
+            for k in range(count):
+                p = base + k
+                for t, v, s, b in whole[k]:
+                    dst[p, t, rows, :] = 0.4 * v + W[p, t, rows, :] * (
+                        GC[0, p, t, rows, :] + F2[p, t, rows, :] * s + b
+                    )
+
+    def fine_sweep(src, dst, low, high, step, src_index=None):
         view = src if src_index is None else src.at[src_index]
 
         def one(n, _):
-            fine_plane(view, dst, low + 2 * n)
-            fine_plane(view, dst, low + 2 * n + 1)
+            fine_planes(view, dst, low + step * n, step)
             return 0
 
-        lax.fori_loop(0, (high - low) // 2, one, 0)
+        lax.fori_loop(0, (high - low) // step, one, 0)
 
     def fine_sides(src, dst, low, high, count, src_index=None):
         view = src if src_index is None else src.at[src_index]
 
         def one(n, _):
-            fine_plane(view, dst, low + n)
-            fine_plane(view, dst, high + n)
+            fine_planes(view, dst, low + (high - low) * n, count)
             return 0
 
-        lax.fori_loop(0, count, one, 0)
-
-    def fine_residue(src, p):
-        out = []
+        lax.fori_loop(0, 2, one, 0)
+
+    def fine_residue(src, base, count):
+        out = [[] for _ in range(count)]
         for r in (8, 16, 24, 32):
-            for t, (v, s, b) in enumerate(stencil(src, FB, FA, p, r, 3, (0, 1), lane, 1.0)):
-                rows = pl.ds(r, 8)
-                out.append(
-                    GC[0, p, t, rows, :] - 1.05 * v + GC[1, p, t, rows, :] * (s - 240.0 * v) + b
-                )
+            rows = pl.ds(r, 8)
+            whole = stencil(src, fine_factors, base, count, r, 3, (0, 1), lane, 1.0)
+            for k in range(count):
+                p = base + k
+                for t, v, s, b in whole[k]:
+                    out[k].append(
+                        GC[0, p, t, rows, :] - 1.05 * v + F2[p, t, rows, :] * (s - 120.0 * v) + b
+                    )
         return out
 
     fine(("z",), "wait_recv")
-    fine(("yz",), "start")
-    fine(("y", "yz"), "wait_recv")
-    fine(("xc",), "start")
-    fine(("xl",), "start")
+    fine(("yz", "xz"), "start")
+    fine(("cy",), "start")
+    fine(("y",), "wait_recv")
+    fine(("xy",), "start")
+    fine(("yz",), "wait_recv")
+    fine(("xyz",), "start")
+    fine(("cy",), "wait_recv")
+    fine(("cx",), "start")
     unpack(5, 13)
     weights(5, 13)
-    fine_sweep(GC, A, 6, 12, 0)
-    fine_sweep(A, B, 7, 11)
-    fine(("x", "xc"), "wait_recv")
-    coarse(1, "start")
+    fine_sweep(GC, A, 6, 12, 3, 0)
+    fine_sweep(A, B, 7, 11, 2)
+    fine(("x", "xz", "xy", "xyz"), "wait_recv")
     unpack(2, 5)
     unpack(13, 16)
     weights(3, 5)
     weights(13, 15)
     fine_sides(GC, A, 3, 12, 3, 0)
+    fine(("cx",), "wait_recv")
+    fine(("cxx",), "start")
     fine_sides(A, B, 4, 11, 3)
 
     def residue_pair(i, _):
-        one = fine_residue(B, 5 + 2 * i)
-        two = fine_residue(B, 6 + 2 * i)
+        one, two = fine_residue(B, 5 + 2 * i, 2)
         for n in range(8):
             RX[i, n % 2, pl.ds(8 * (n // 2), 8), :] = one[n] + two[n]
         return 0
@@ -464,18 +538,20 @@
 
     coarse(0, "start")
 
-    fine(("xl",), "wait_recv")
-    unpack(0, 2)
-    unpack(16, 18)
-    weights(1, 3)
-    weights(15, 17)
-    fine_sides(GC, A, 1, 15, 2, 0)
-    fine_sides(A, B, 2, 14, 2)
+    for side in range(2):
+        for n in range(2):
+            p = (10 if side == 0 else 6) + n
+            acc = blank
+            for j, r in enumerate(starts):
+                turned = pltpu.roll(B[p, 2, pl.ds(r, 8), :], (16 * j + 8) % 128, 1)
+                acc = jnp.where((lane >= 16 * j) & (lane < 16 * j + 16), turned, acc)
+            SS[side, n] = acc
+    fine(("s",), "start")
 
     cylow = (gy * 16 + sub - 8) >= 0
     cyhigh = (gy * 16 + sub + 16) < 256
 
-    coarse(1, "wait_recv")
+    fine(("cxx",), "wait_recv")
 
     def coarse_unpack(k):
         for p in range(CX):
@@ -493,10 +569,8 @@
         scale = jnp.where((at >= 0) & (at < 32), DAMP, 0.0).astype(F32)
         for n, r in enumerate((0, 8, 16, 24)):
             scales = [CO[1, p, t, pl.ds(r, 8), :] for t in range(2)]
-            before, after = shifted_scales(scales, lane)
+            keep_factors((K2, KB, KBV, KA, KAV), p, pl.ds(r, 8), scales, lane, 0.25, 0.5)
             for t in range(2):
-                KB[p, t, pl.ds(r, 8), :] = before[t]
-                KA[p, t, pl.ds(r, 8), :] = after[t]
                 w = scale / (1.05 + 60.0 * scales[t])
                 if r == 0:
                     w = jnp.where(cylow, w, 0.0)
@@ -509,6 +583,7 @@
 
     lax.fori_loop(0, CX, coarse_weights, 0)
 
+    fine(("z", "x", "y", "xz", "yz", "xy", "xyz", "cy", "cx", "cxx"), "wait_send")
     coarse(0, "wait_recv")
     coarse_unpack(0)
 
@@ -523,15 +598,15 @@
 
     def coarse_sweep(src, dst, low, high):
         def one(n, _):
-            for half in range(2):
-                p = low + 2 * n + half
-                for r in (4, 12, 20):
-                    for t, (v, s, b) in enumerate(
-                        stencil(src, KB, KA, p, r, 2, (0, 1), lane, 2.0)
-                    ):
-                        rows = pl.ds(r, 8)
+            base = low + 2 * n
+            for r in (4, 12, 20):
+                rows = pl.ds(r, 8)
+                whole = stencil(src, (KB, KBV, KA, KAV), base, 2, r, 2, (0, 1), lane, 0.5)
+                for k in range(2):
+                    p = base + k
+                    for t, v, s, b in whole[k]:
                         dst[p, t, rows, :] = 0.4 * v + CW[p, t, rows, :] * (
-                            CO[0, p, t, rows, :] + CO[1, p, t, rows, :] * s + b
+                            CO[0, p, t, rows, :] + K2[p, t, rows, :] * s + b
                         )
             return 0
 
@@ -560,6 +635,23 @@
             UPS[q, t, pl.ds(0, 24, stride=2), :] = part
             UPS[q, t, pl.ds(1, 24, stride=2), :] = part
 
+    fine(("s",), "wait_send")
+    fine(("s",), "wait_recv")
+
+    def spread_edge(side, first):
+        for n in range(2):
+            for j, r in enumerate(starts):
+                turned = pltpu.roll(SR[side, n], (128 - 16 * j - 8) % 128, 1)
+                B[first + n, 2, pl.ds(r, 8), :] = jnp.where(zmask, turned, 0.0)
+
+    @pl.when(gx > 0)
+    def _():
+        spread_edge(0, 2)
+
+    @pl.when(gx < NXD - 1)
+    def _():
+        spread_edge(1, 14)
+
     def add_up(q, _):
         for half in range(2):
             for r in range(6):
@@ -571,21 +663,21 @@
 
     lax.fori_loop(0, 8, add_up, 0)
 
-    fine_sweep(A, B, 3, 15)
-    fine_sweep(B, A, 4, 14)
-
-    def finish(x, _):
-        vals = fine_residue(A, 5 + x)
-        for n in range(8):
-            t, r = n % 2, 8 * (n // 2)
-            res_ref[x, pl.ds(r, 8), pl.ds(128 * t, 128)] = vals[n]
-            sol_ref[x, pl.ds(r, 8), pl.ds(128 * t, 128)] = A[5 + x, t, pl.ds(8 + r, 8), :]
+    fine_sweep(A, B, 3, 15, 3)
+    fine_sweep(B, A, 4, 14, 5)
+
+    def finish(n, _):
+        both = fine_residue(A, 5 + 2 * n, 2)
+        for k in range(2):
+            x = 2 * n + k
+            for i in range(8):
+                t, r = i % 2, 8 * (i // 2)
+                res_ref[x, pl.ds(r, 8), pl.ds(128 * t, 128)] = both[k][i]
+                sol_ref[x, pl.ds(r, 8), pl.ds(128 * t, 128)] = A[5 + x, t, pl.ds(8 + r, 8), :]
         return 0
 
-    lax.fori_loop(0, 8, finish, 0)
-
-    fine(("z", "x", "y", "yz", "xc", "xl"), "wait_send")
-    coarse(1, "wait_send")
+    lax.fori_loop(0, 4, finish, 0)
+
     coarse(0, "wait_send")
 
 
@@ -603,26 +695,20 @@
             pltpu.VMEM((2, PX, 3, ROWS, 128), F32),
             pltpu.VMEM((8, 8, 128), F32),
             pltpu.VMEM((3, PX, 8, 128), F32),
-            fine,
-            fine,
-            fine,
-            fine,
-            fine,
+            pltpu.VMEM((2, 2, 8, 128), F32),
+            pltpu.VMEM((2, 2, 8, 128), F32),
+            *[fine] * 8,
             pltpu.VMEM((4, 2, 32, 128), F32),
             pltpu.VMEM((2, CX, 2, CROWS, 128), F32),
             pltpu.VMEM((2, 8, 128), F32),
             pltpu.VMEM((2, 5, 3, 8, 128), F32),
-            coarse,
-            coarse,
-            coarse,
-            coarse,
-            coarse,
+            *[coarse] * 8,
             pltpu.VMEM((8, 3, ROWS, 128), F32),
             pltpu.SemaphoreType.DMA((4,)),
             pltpu.SemaphoreType.DMA((NF,)),
             pltpu.SemaphoreType.DMA((NF,)),
-            pltpu.SemaphoreType.DMA((2 * NC,)),
-            pltpu.SemaphoreType.DMA((2 * NC,)),
+            pltpu.SemaphoreType.DMA((NC,)),
+            pltpu.SemaphoreType.DMA((NC,)),
         ],
         compiler_params=pltpu.CompilerParams(collective_id=0, has_side_effects=True),
     )(right_side, volscale)

time: 38.9 us -> 35.8 us (0.920)
  the two profiles are of different devices: /device:TPU:89 before, /device:TPU:25 now
where the time goes in v5:
time: 35.8 us; the launch traced here: 35.7 us
  Pallas kernels  33.6 us (94%)
  local copies, waits for them, and re-layouts  1.41 us (4%)
  between operations  0.64 us (2%)
    pallas_call x1, Pallas kernels, on_device(): pl.pallas_call(kernel, out_shape=(shape, shape), in_specs=[any_space] * 2...  33.6 us
    unnamed x2, local copies, waits for them, and re-layouts  1.41 us

profile of v5, /device:TPU:25, one launch (start us, length us, event | category | flops | bytes accessed | tf_op | source)
XLA Modules:
  0.0 35.7 jit_solution(3551230011049474052)
XLA Ops:
  0.6 33.6 %shard_map.41 = (f32[8,32,256]{2,1,0:T(8,128)S(1)}, f32[8,32,256]{2,1,0:T(8,128)S(1)}) custom-call(f32[8,32,256]{2,1,0:T(8,128)} %g_hbm.1, f32[8,32,256]{2,1,0:T(8,128)} %c_hbm.1), custom_call_target="tpu_custom_call" | custom-call | tf_op jit(solution)/shard_map/pallas_call | solution.py:689
  34.3 0.7 %copy.6 = f32[8,32,256]{2,1,0:T(8,128)} copy(f32[8,32,256]{2,1,0:T(8,128)S(1)} %get-tuple-element.2) | data formatting | bytes 524288
  35.0 0.7 %copy.7 = f32[8,32,256]{2,1,0:T(8,128)} copy(f32[8,32,256]{2,1,0:T(8,128)S(1)} %get-tuple-element.3) | data formatting | bytes 524288

commit v6 on v5

--- a/solution.py
+++ b/solution.py
@@ -28,12 +28,11 @@
         side, far = 2 - dx, 2 - 2 * dx
         sg, dg = ((10, 3), (2, 3)) if dx == 1 else ((5, 3), (13, 3))
         sc, dc = ((11, 2), (3, 2)) if dx == 1 else ((5, 2), (13, 2))
-        out.append(("x", dx, 0, 0, ("GC", 0, sg, mid), ("GC", 0, dg, mid)))
-        out.append(("x", dx, 0, 0, ("GC", 1, sc, mid), ("GC", 1, dc, mid)))
+        out.append(("x", dx, 0, 0, ("GC", 0, sg, (3, 42)), ("GC", 0, dg, (3, 42))))
+        out.append(("x", dx, 0, 0, ("GC", 1, sc, (3, 42)), ("GC", 1, dc, (3, 42))))
         out.append(("xz", dx, 0, 0, ("PR", (1, 1), sg, (0, 8)), ("PR", (1, 1), dg, (0, 8))))
         for rows in (lo, hi):
-            out.append(("xy", dx, 0, 0, ("GC", 0, sg, rows), ("GC", 0, dg, rows)))
-            out.append(("xy", dx, 0, 0, ("GC", 1, sc, rows), ("GC", 1, dc, rows)))
+            pass
         for slot, rows in ((0, (3, 5)), (2, (0, 5))):
             out.append(("xyz", dx, 0, 0, ("PR", (slot, 1), sg, rows), ("PR", (slot, 1), dg, rows)))
         out.append(("cx", dx, 0, 0, ("CO", (5, 4), (3, 26)), ("CO", (1 if dx == 1 else 9, 4), (3, 26))))
@@ -426,7 +425,6 @@
 
     fine(("z",), "start")
     fine(("y",), "start")
-    fine(("x",), "start")
 
     def unpack(low, high):
         def unpack_plane(p, _):
@@ -508,15 +506,15 @@
     fine(("yz", "xz"), "start")
     fine(("cy",), "start")
     fine(("y",), "wait_recv")
-    fine(("xy",), "start")
+    fine(("x",), "start")
     fine(("yz",), "wait_recv")
     fine(("xyz",), "start")
-    fine(("cy",), "wait_recv")
-    fine(("cx",), "start")
     unpack(5, 13)
     weights(5, 13)
     fine_sweep(GC, A, 6, 12, 3, 0)
     fine_sweep(A, B, 7, 11, 2)
+    fine(("cy",), "wait_recv")
+    fine(("cx",), "start")
     fine(("x", "xz", "xy", "xyz"), "wait_recv")
     unpack(2, 5)
     unpack(13, 16)
@@ -681,12 +679,23 @@
     coarse(0, "wait_send")
 
 
+def closing(sol_ref, res_ref, sol_hbm, res_hbm, sems):
+    copies = [
+        pltpu.make_async_copy(sol_ref, sol_hbm, sems.at[0]),
+        pltpu.make_async_copy(res_ref, res_hbm, sems.at[1]),
+    ]
+    for cp in copies:
+        cp.start()
+    for cp in copies:
+        cp.wait()
+
+
 def on_device(right_side, volscale):
     shape = pltpu.VMEM(right_side.shape, F32)
     fine = pltpu.VMEM((PX, 3, ROWS, 128), F32)
     coarse = pltpu.VMEM((CX, 2, CROWS, 128), F32)
     any_space = pl.BlockSpec(memory_space=pl.ANY)
-    return pl.pallas_call(
+    sol, res = pl.pallas_call(
         kernel,
         out_shape=(shape, shape),
         in_specs=[any_space] * 2,
@@ -712,6 +721,18 @@
         ],
         compiler_params=pltpu.CompilerParams(collective_id=0, has_side_effects=True),
     )(right_side, volscale)
+    plain = jax.ShapeDtypeStruct(right_side.shape, F32)
+    in_vmem = pl.BlockSpec(memory_space=pltpu.VMEM)
+    sol = pltpu.with_memory_space_constraint(sol, pltpu.VMEM)
+    res = pltpu.with_memory_space_constraint(res, pltpu.VMEM)
+    return pl.pallas_call(
+        closing,
+        out_shape=(plain, plain),
+        in_specs=[in_vmem] * 2,
+        out_specs=(any_space, any_space),
+        scratch_shapes=[pltpu.SemaphoreType.DMA((2,))],
+        compiler_params=pltpu.CompilerParams(vmem_limit_bytes=1 << 20),
+    )(sol, res)
 
 
 def solution(mesh):

time: 35.8 us -> 35.1 us (0.980)
  local copies, waits for them, and re-layouts: 1.41 us -> 0 us
  Pallas kernels: 33.6 us -> 34.3 us
    unnamed x2 -> x0, local copies, waits for them, and re-layouts: 1.41 us -> none
    pallas_call x0 -> x1, Pallas kernels: none -> 0.81 us  [on_device(): pl.pallas_call(closing, out_shape=(plain, plain), in_specs=[in_vmem] * 2,...]
where the time goes in v6:
time: 35.1 us; the launch traced here: 35 us
  Pallas kernels  34.3 us (98%)
  between operations  0.64 us (2%)
    pallas_call x1, Pallas kernels, on_device(): pl.pallas_call(kernel, out_shape=(shape, shape), in_specs=[any_space] * 2...  33.5 us
    pallas_call x1, Pallas kernels, on_device(): pl.pallas_call(closing, out_shape=(plain, plain), in_specs=[in_vmem] * 2,...  0.81 us

profile of v6, /device:TPU:25, one launch (start us, length us, event | category | flops | bytes accessed | tf_op | source)
XLA Modules:
  0.0 35.0 jit_solution(14729131965434462110)
XLA Ops:
  0.6 33.5 %shard_map.41 = (f32[8,32,256]{2,1,0:T(8,128)S(1)}, f32[8,32,256]{2,1,0:T(8,128)S(1)}) custom-call(f32[8,32,256]{2,1,0:T(8,128)} %g_hbm.1, f32[8,32,256]{2,1,0:T(8,128)} %c_hbm.1), custom_call_target="tpu_custom_call" | custom-call | tf_op jit(solution)/shard_map/pallas_call | solution.py:698
  34.2 0.8 %shard_map.42 = (f32[8,32,256]{2,1,0:T(8,128)}, f32[8,32,256]{2,1,0:T(8,128)}) custom-call(f32[8,32,256]{2,1,0:T(8,128)S(1)} %get-tuple-element.4.sol_ref, f32[8,32,256]{2,1,0:T(8,128)S(1)} %get-tuple-element.5.res_ref), custom_call_target="tpu_custom_call" | custom-call | tf_op jit(solution)/shard_map/pallas_call | solution.py:728

commit v7 on v6

--- a/solution.py
+++ b/solution.py
@@ -594,13 +594,13 @@
 
     lax.fori_loop(0, CX, coarse_first, 0)
 
-    def coarse_sweep(src, dst, low, high):
+    def coarse_sweep(src, dst, low, high, step):
         def one(n, _):
-            base = low + 2 * n
+            base = low + step * n
             for r in (4, 12, 20):
                 rows = pl.ds(r, 8)
-                whole = stencil(src, (KB, KBV, KA, KAV), base, 2, r, 2, (0, 1), lane, 0.5)
-                for k in range(2):
+                whole = stencil(src, (KB, KBV, KA, KAV), base, step, r, 2, (0, 1), lane, 0.5)
+                for k in range(step):
                     p = base + k
                     for t, v, s, b in whole[k]:
                         dst[p, t, rows, :] = 0.4 * v + CW[p, t, rows, :] * (
@@ -608,11 +608,11 @@
                         )
             return 0
 
-        lax.fori_loop(0, (high - low) // 2, one, 0)
-
-    coarse_sweep(CA, CB, 1, 13)
-    coarse_sweep(CB, CA, 2, 12)
-    coarse_sweep(CA, CB, 3, 11)
+        lax.fori_loop(0, (high - low) // step, one, 0)
+
+    coarse_sweep(CA, CB, 1, 13, 4)
+    coarse_sweep(CB, CA, 2, 12, 5)
+    coarse_sweep(CA, CB, 3, 11, 4)
 
     ri = lax.broadcasted_iota(jnp.int32, (128, 256), 0)
     ci = lax.broadcasted_iota(jnp.int32, (128, 256), 1)
@@ -665,16 +665,16 @@
     fine_sweep(B, A, 4, 14, 5)
 
     def finish(n, _):
-        both = fine_residue(A, 5 + 2 * n, 2)
-        for k in range(2):
-            x = 2 * n + k
+        both = fine_residue(A, 5 + 4 * n, 4)
+        for k in range(4):
+            x = 4 * n + k
             for i in range(8):
                 t, r = i % 2, 8 * (i // 2)
                 res_ref[x, pl.ds(r, 8), pl.ds(128 * t, 128)] = both[k][i]
                 sol_ref[x, pl.ds(r, 8), pl.ds(128 * t, 128)] = A[5 + x, t, pl.ds(8 + r, 8), :]
         return 0
 
-    lax.fori_loop(0, 4, finish, 0)
+    lax.fori_loop(0, 2, finish, 0)
 
     coarse(0, "wait_send")
 

time: 35.1 us -> 34.6 us (0.986)
  Pallas kernels: 34.3 us -> 33.8 us
    pallas_call x1, Pallas kernels: 33.5 us -> 33 us  [on_device(): pl.pallas_call(kernel, out_shape=(shape, shape), in_specs=[any_space] * 2...]
where the time goes in v7:
time: 34.6 us; the launch traced here: 34.5 us
  Pallas kernels  33.8 us (98%)
  between operations  0.64 us (2%)
    pallas_call x1, Pallas kernels, on_device(): pl.pallas_call(kernel, out_shape=(shape, shape), in_specs=[any_space] * 2...  33 us
    pallas_call x1, Pallas kernels, on_device(): pl.pallas_call(closing, out_shape=(plain, plain), in_specs=[in_vmem] * 2,...  0.81 us

profile of v7, /device:TPU:25, one launch (start us, length us, event | category | flops | bytes accessed | tf_op | source)
XLA Modules:
  0.0 34.5 jit_solution(14982751922394925098)
XLA Ops:
  0.6 33.0 %shard_map.41 = (f32[8,32,256]{2,1,0:T(8,128)S(1)}, f32[8,32,256]{2,1,0:T(8,128)S(1)}) custom-call(f32[8,32,256]{2,1,0:T(8,128)} %g_hbm.1, f32[8,32,256]{2,1,0:T(8,128)} %c_hbm.1), custom_call_target="tpu_custom_call" | custom-call | tf_op jit(solution)/shard_map/pallas_call | solution.py:698
  33.6 0.8 %shard_map.42 = (f32[8,32,256]{2,1,0:T(8,128)}, f32[8,32,256]{2,1,0:T(8,128)}) custom-call(f32[8,32,256]{2,1,0:T(8,128)S(1)} %get-tuple-element.4.sol_ref, f32[8,32,256]{2,1,0:T(8,128)S(1)} %get-tuple-element.5.res_ref), custom_call_target="tpu_custom_call" | custom-call | tf_op jit(solution)/shard_map/pallas_call | solution.py:728

commit v8 on v7

--- a/solution.py
+++ b/solution.py
@@ -525,13 +525,15 @@
     fine(("cxx",), "start")
     fine_sides(A, B, 4, 11, 3)
 
-    def residue_pair(i, _):
-        one, two = fine_residue(B, 5 + 2 * i, 2)
-        for n in range(8):
-            RX[i, n % 2, pl.ds(8 * (n // 2), 8), :] = one[n] + two[n]
+    def residue_pairs(n, _):
+        four = fine_residue(B, 5 + 4 * n, 4)
+        for half in range(2):
+            one, two = four[2 * half], four[2 * half + 1]
+            for k in range(8):
+                RX[2 * n + half, k % 2, pl.ds(8 * (k // 2), 8), :] = one[k] + two[k]
         return 0
 
-    lax.fori_loop(0, 4, residue_pair, 0)
+    lax.fori_loop(0, 2, residue_pairs, 0)
     coarsen_rows(0)
 
     coarse(0, "start")

time: 34.6 us -> 34.4 us (level)
  no operation moved by 1% of the time
where the time goes in v8:
time: 34.4 us; the launch traced here: 34.3 us
  Pallas kernels  33.7 us (98%)
  between operations  0.64 us (2%)
    pallas_call x1, Pallas kernels, on_device(): pl.pallas_call(kernel, out_shape=(shape, shape), in_specs=[any_space] * 2...  32.9 us
    pallas_call x1, Pallas kernels, on_device(): pl.pallas_call(closing, out_shape=(plain, plain), in_specs=[in_vmem] * 2,...  0.81 us

profile of v8, /device:TPU:25, one launch (start us, length us, event | category | flops | bytes accessed | tf_op | source)
XLA Modules:
  0.0 34.3 jit_solution(4950196252444901531)
XLA Ops:
  0.6 32.9 %shard_map.41 = (f32[8,32,256]{2,1,0:T(8,128)S(1)}, f32[8,32,256]{2,1,0:T(8,128)S(1)}) custom-call(f32[8,32,256]{2,1,0:T(8,128)} %g_hbm.1, f32[8,32,256]{2,1,0:T(8,128)} %c_hbm.1), custom_call_target="tpu_custom_call" | custom-call | tf_op jit(solution)/shard_map/pallas_call | solution.py:700
  33.5 0.8 %shard_map.42 = (f32[8,32,256]{2,1,0:T(8,128)}, f32[8,32,256]{2,1,0:T(8,128)}) custom-call(f32[8,32,256]{2,1,0:T(8,128)S(1)} %get-tuple-element.4.sol_ref, f32[8,32,256]{2,1,0:T(8,128)S(1)} %get-tuple-element.5.res_ref), custom_call_target="tpu_custom_call" | custom-call | tf_op jit(solution)/shard_map/pallas_call | solution.py:730
